TPU v7x, 32 devices: a whole 2x2x4 slice. The times are simulated.
32 devices in a mesh: fsdp: 16 (over z, y, core), tensor: 2 (over x).
Axes of the slice: x: 2, y: 2, z: 4, core: 2. Of those that a mesh axis runs over, the one named last changes fastest.
Arguments:
- embedded: bfloat16 [8192, 768], P(('fsdp', 'tensor')), may hold values from -6 to 6
- segments: int32 [32, 256], P('fsdp'), may hold values from 0 to 3, never falling along the last dimension, each value on 1 to 128 neighbouring positions
- thoughts: int32 [32, 64], P(('fsdp', 'tensor')), may hold values from -1 to 255, as said below
- cotangent: bfloat16 [8192, 768], P(('fsdp', 'tensor')), may hold values from -6 to 6
- norm_gains: bfloat16 [2, 2, 768], replicated, may hold values from 0.5 to 1.5
- norm_shifts: bfloat16 [2, 2, 768], replicated, may hold values from -1 to 1
- joint_weight: bfloat16 [2, 768, 3, 768], P(None, 'fsdp', None, 'tensor'), may hold values from -0.21875 to 0.21875
- joint_bias: bfloat16 [2, 2, 768], P(None, None, 'tensor'), may hold values from -1 to 1
- merge_weight: bfloat16 [2, 768, 768], P(None, 'tensor', 'fsdp'), may hold values from -0.875 to 0.875
- expand_weight: bfloat16 [2, 768, 3072], P(None, 'fsdp', 'tensor'), may hold values from -0.21875 to 0.21875
- expand_bias: bfloat16 [2, 3072], P(None, 'tensor'), may hold values from -1 to 1
- shrink_weight: bfloat16 [2, 3072, 768], P(None, 'tensor', 'fsdp'), may hold values from -0.109375 to 0.109375
- branch_biases: bfloat16 [2, 2, 768], replicated, may hold values from -1 to 1
Outputs:
- latent_out: bfloat16 [8192, 768], P(('fsdp', 'tensor'))
- language_out: bfloat16 [8192, 768], P(('fsdp', 'tensor'))
- embedded_grad: float32 [8192, 768], P(('fsdp', 'tensor'))
- gains_grad: float32 [2, 2, 768], replicated
- shifts_grad: float32 [2, 2, 768], replicated
- joint_grad: float32 [2, 768, 3, 768], P(None, 'fsdp', None, 'tensor')
- joint_bias_grad: float32 [2, 2, 768], P(None, None, 'tensor')
- merge_grad: float32 [2, 768, 768], P(None, 'tensor', 'fsdp')
- expand_grad: float32 [2, 768, 3072], P(None, 'fsdp', 'tensor')
- expand_bias_grad: float32 [2, 3072], P(None, 'tensor')
- shrink_grad: float32 [2, 3072, 768], P(None, 'tensor', 'fsdp')
- branch_grad: float32 [2, 2, 768], replicated
Inputs may be any that keep to these rules, and one draw needn't show every extreme that they name: `segments`: within a sequence the document numbers never fall; a document spans 1 to 128 positions, and some document spans exactly 128. `thoughts`: each row lists distinct positions of its sequence, at least 1, in its used entries, followed by -1 in the unused ones; every row uses 64 // 2 entries or more, and the first row uses all 64.
All inputs are finite; a program needn't handle non-finite values.
Results may differ from a plain program's by a relative error of at most 0.02.
Values may be sent and summed in bfloat16 or wider, within the bound.
No kernel may reach another device: no remote copies, remote signals or barrier semaphores. Data moves between devices by JAX's collectives and lax.ppermute only.
A program may use at most 128 MiB of HBM per device.

v0:
```python
from functools import partial

import jax
import jax.numpy as jnp
from jax import lax
from jax.sharding import PartitionSpec as P

HEAD = 64


EPSILON = 1e-05


def layer_norm(rows, gain, shift):
    center = rows - jnp.mean(rows, axis=-1, keepdims=True)
    spread = jnp.mean(center * center, axis=-1, keepdims=True)
    return center * lax.rsqrt(spread + EPSILON) * gain + shift


def gather_rows(rows):
    return lax.all_gather(rows, "tensor", axis=0, tiled=True)


def scatter_rows(source, weight, pattern):
    return lax.psum_scatter(
        jnp.einsum(pattern, source, weight, preferred_element_type=jnp.float32).astype(
            jnp.bfloat16
        ),
        "tensor",
        scatter_dimension=0,
        tiled=True,
    ).astype(jnp.float32)


def fetch_weights(joint, merge, expand, shrink):
    return (
        lax.all_gather(joint, "fsdp", axis=0, tiled=True),
        lax.all_gather(merge, "fsdp", axis=1, tiled=True),
        lax.all_gather(expand, "fsdp", axis=0, tiled=True),
        lax.all_gather(shrink, "fsdp", axis=1, tiled=True),
    )


def reduce_weights(matrices):
    return (
        lax.psum_scatter(matrices[0], "fsdp", scatter_dimension=0, tiled=True),
        lax.psum_scatter(matrices[1], "fsdp", scatter_dimension=1, tiled=True),
        lax.psum_scatter(matrices[2], "fsdp", scatter_dimension=0, tiled=True),
        lax.psum_scatter(matrices[3], "fsdp", scatter_dimension=1, tiled=True),
    )


def block_scores(query, keys, segments, start, block):
    seq_len = segments.shape[1]
    width = query.shape[1]
    heads = width // HEAD
    which = start // seq_len
    first = which * seq_len
    rows_q = lax.dynamic_slice_in_dim(query, start, block, 0).reshape(block, heads, HEAD)
    rows_k = lax.dynamic_slice_in_dim(keys, first, seq_len, 0).reshape(seq_len, heads, HEAD)
    scores = jnp.einsum(
        "qhd,khd->hqk", rows_q, rows_k, preferred_element_type=jnp.float32
    ) * HEAD ** (-0.5)
    row_segments = lax.dynamic_slice_in_dim(segments, which, 1, 0)[0]
    local = start - first
    query_places = local + jnp.arange(block)
    key_places = jnp.arange(seq_len)
    allowed = (row_segments[:, None] == row_segments[None, :]) & (
        key_places[None, :] <= query_places[:, None]
    )
    return (jnp.where(allowed[None], scores, -1e30), rows_q, rows_k, first)


def attend_forward(query, keys, values, segments, block):
    total = query.shape[0]
    seq_len = segments.shape[1]
    width = query.shape[1]
    heads = width // HEAD

    def one_block(index):
        start = index * block
        scores, rows_q, rows_k, first = block_scores(query, keys, segments, start, block)
        rows_v = lax.dynamic_slice_in_dim(values, first, seq_len, 0).reshape(seq_len, heads, HEAD)
        peak = jnp.max(scores, axis=-1, keepdims=True)
        exponent = jnp.exp(scores - peak)
        weight_sum = jnp.sum(exponent, axis=-1, keepdims=True)
        attend = (exponent / weight_sum).astype(jnp.bfloat16)
        output = jnp.einsum("hqk,khd->qhd", attend, rows_v, preferred_element_type=jnp.float32)
        return (output.reshape(block, width), (peak + jnp.log(weight_sum))[..., 0])

    outputs, logsum = lax.map(one_block, jnp.arange(total // block))
    return (outputs.reshape(total, width), logsum)


def attend_backward(query, keys, values, segments, logsum, grad_mixed, block):
    total = query.shape[0]
    seq_len = segments.shape[1]
    width = query.shape[1]
    heads = width // HEAD

    def step(carry, index):
        grad_keys, grad_values = carry
        start = index * block
        scores, rows_q, rows_k, first = block_scores(query, keys, segments, start, block)
        rows_v = lax.dynamic_slice_in_dim(values, first, seq_len, 0).reshape(seq_len, heads, HEAD)
        rows_g = lax.dynamic_slice_in_dim(grad_mixed, start, block, 0).reshape(block, heads, HEAD)
        probs_full = jnp.exp(scores - logsum[index][..., None])
        attend = probs_full.astype(jnp.bfloat16)
        grad_probs = jnp.einsum("qhd,khd->hqk", rows_g, rows_v, preferred_element_type=jnp.float32)
        inner = jnp.sum(grad_probs * probs_full, axis=-1, keepdims=True)
        grad_scores = (probs_full * (grad_probs - inner) * HEAD ** (-0.5)).astype(jnp.bfloat16)
        grad_query = jnp.einsum(
            "hqk,khd->qhd", grad_scores, rows_k, preferred_element_type=jnp.float32
        )
        more_keys = jnp.einsum(
            "hqk,qhd->khd", grad_scores, rows_q, preferred_element_type=jnp.float32
        ).reshape(seq_len, width)
        more_values = jnp.einsum(
            "hqk,qhd->khd", attend, rows_g, preferred_element_type=jnp.float32
        ).reshape(seq_len, width)
        old_keys = lax.dynamic_slice_in_dim(grad_keys, first, seq_len, 0)
        old_values = lax.dynamic_slice_in_dim(grad_values, first, seq_len, 0)
        grad_keys = lax.dynamic_update_slice_in_dim(grad_keys, old_keys + more_keys, first, 0)
        grad_values = lax.dynamic_update_slice_in_dim(
            grad_values, old_values + more_values, first, 0
        )
        return ((grad_keys, grad_values), grad_query.reshape(block, width))

    zeros_start = jnp.zeros((total, width), jnp.float32)
    (grad_keys, grad_values), grad_query = lax.scan(
        step, (zeros_start, zeros_start), jnp.arange(total // block)
    )
    return (grad_query.reshape(total, width), grad_keys, grad_values)


def layer_forward(rows, gains, shifts, pair_bias, expand_shift, biases, fetched, segments):
    joint, merge, expand, shrink = fetched
    block = min(512, segments.shape[1])
    normed = layer_norm(rows, gains[0], shifts[0])
    first_rows = gather_rows(normed.astype(jnp.bfloat16))
    joint_out = jnp.einsum("rd,dch->rch", first_rows, joint, preferred_element_type=jnp.float32)
    query = (joint_out[:, 0] + pair_bias[0]).astype(jnp.bfloat16)
    keys = joint_out[:, 1].astype(jnp.bfloat16)
    values = (joint_out[:, 2] + pair_bias[1]).astype(jnp.bfloat16)
    mixed, logsum = attend_forward(query, keys, values, segments, block)
    mixed = mixed.astype(jnp.bfloat16)
    middle = rows + scatter_rows(mixed, merge, "rh,hd->rd") + biases[0]
    normed_two = layer_norm(middle, gains[1], shifts[1])
    second_rows = gather_rows(normed_two.astype(jnp.bfloat16))
    hidden = jnp.dot(second_rows, expand, preferred_element_type=jnp.float32) + expand_shift
    active = jax.nn.gelu(hidden, approximate=True).astype(jnp.bfloat16)
    result = middle + scatter_rows(active, shrink, "rf,fd->rd") + biases[1]
    saved = (
        rows,
        middle,
        first_rows,
        second_rows,
        query,
        keys,
        values,
        logsum,
        mixed,
        hidden,
        active,
    )
    return (result, saved)


def layer_backward(grad_result, saved, gains, shifts, fetched, segments):
    joint, merge, expand, shrink = fetched
    rows, middle, first_rows, second_rows, query, keys, values, logsum, mixed, hidden, active = (
        saved
    )
    block = min(512, segments.shape[1])
    _, gelu_pull = jax.vjp(partial(jax.nn.gelu, approximate=True), hidden)
    grad_rows_out = gather_rows(grad_result.astype(jnp.bfloat16))
    grad_shrink = jnp.einsum("rf,rd->fd", active, grad_rows_out, preferred_element_type=jnp.float32)
    grad_active = jnp.einsum("rd,fd->rf", grad_rows_out, shrink, preferred_element_type=jnp.float32)
    grad_hidden = gelu_pull(grad_active)[0]
    expand_shift_grad = jnp.sum(grad_hidden, axis=0)
    grad_hidden = grad_hidden.astype(jnp.bfloat16)
    grad_expand = jnp.einsum(
        "rd,rf->df", second_rows, grad_hidden, preferred_element_type=jnp.float32
    )
    grad_normed_two = scatter_rows(grad_hidden, expand, "rf,df->rd")
    _, norm_pull_two = jax.vjp(layer_norm, middle, gains[1], shifts[1])
    grad_middle, gain_two, shift_two = norm_pull_two(grad_normed_two)
    grad_middle = grad_middle + grad_result
    shrink_shift_grad = jnp.sum(grad_result, axis=0)
    merge_shift_grad = jnp.sum(grad_middle, axis=0)
    grad_rows_mid = gather_rows(grad_middle.astype(jnp.bfloat16))
    grad_merge = jnp.einsum("rh,rd->hd", mixed, grad_rows_mid, preferred_element_type=jnp.float32)
    grad_mixed = jnp.einsum(
        "rd,hd->rh", grad_rows_mid, merge, preferred_element_type=jnp.float32
    ).astype(jnp.bfloat16)
    grad_query, grad_keys, grad_values = attend_backward(
        query, keys, values, segments, logsum, grad_mixed, block
    )
    pair_grad = jnp.stack((jnp.sum(grad_query, axis=0), jnp.sum(grad_values, axis=0)))
    grad_joint_out = jnp.stack((grad_query, grad_keys, grad_values), axis=1).astype(jnp.bfloat16)
    grad_joint = jnp.einsum(
        "rd,rch->dch", first_rows, grad_joint_out, preferred_element_type=jnp.float32
    )
    grad_normed = scatter_rows(grad_joint_out, joint, "rch,dch->rd")
    _, norm_pull_one = jax.vjp(layer_norm, rows, gains[0], shifts[0])
    grad_rows, gain_one, shift_one = norm_pull_one(grad_normed)
    grad_rows = grad_rows + grad_middle
    vectors = (
        jnp.stack((gain_one, gain_two)),
        jnp.stack((shift_one, shift_two)),
        jnp.stack((merge_shift_grad, shrink_shift_grad)),
    )
    split_terms = (pair_grad, expand_shift_grad)
    matrices = (grad_joint, grad_merge, grad_expand, grad_shrink)
    return (grad_rows, vectors, split_terms, matrices)


def shards(
    embedded,
    segments,
    thoughts,
    cotangent,
    norm_gains,
    norm_shifts,
    joint_weight,
    joint_bias,
    merge_weight,
    expand_weight,
    expand_bias,
    shrink_weight,
    branch_biases,
):
    gains = norm_gains.astype(jnp.float32)
    shifts = norm_shifts.astype(jnp.float32)
    pair_all = joint_bias.astype(jnp.float32)
    expand_all = expand_bias.astype(jnp.float32)
    biases_all = branch_biases.astype(jnp.float32)
    seq_len = embedded.shape[0]
    fetched_one = fetch_weights(
        joint_weight[0], merge_weight[0], expand_weight[0], shrink_weight[0]
    )
    start_rows = embedded.astype(jnp.float32)
    latent, saved_one = layer_forward(
        start_rows,
        gains[0],
        shifts[0],
        pair_all[0],
        expand_all[0],
        biases_all[0],
        fetched_one,
        segments,
    )
    latent_low = latent.astype(jnp.bfloat16)
    places = jnp.arange(seq_len)
    slot_row = thoughts[0]
    slot_cols = (places[:, None] == slot_row[None, :]).astype(jnp.float32)
    source_cols = (places[:, None] == (slot_row - 1)[None, :]).astype(jnp.float32)
    picked = jnp.einsum(
        "ps,pd->sd",
        source_cols.astype(jnp.bfloat16),
        latent_low,
        preferred_element_type=jnp.float32,
    )
    occupied = jnp.sum(slot_cols, axis=1)
    second_in = start_rows * (1.0 - occupied)[:, None] + jnp.dot(
        slot_cols.astype(jnp.bfloat16),
        picked.astype(jnp.bfloat16),
        preferred_element_type=jnp.float32,
    )
    fetched_two = fetch_weights(
        joint_weight[1], merge_weight[1], expand_weight[1], shrink_weight[1]
    )
    language, saved_two = layer_forward(
        second_in,
        gains[1],
        shifts[1],
        pair_all[1],
        expand_all[1],
        biases_all[1],
        fetched_two,
        segments,
    )
    back_two = fetch_weights(joint_weight[1], merge_weight[1], expand_weight[1], shrink_weight[1])
    grad_second, vectors_two, split_two, matrices_two = layer_backward(
        cotangent.astype(jnp.float32), saved_two, gains[1], shifts[1], back_two, segments
    )
    owned_two = reduce_weights(matrices_two)
    grad_picked = jnp.einsum("ps,pd->sd", slot_cols, grad_second, precision=lax.Precision.HIGHEST)
    grad_latent = jnp.dot(source_cols, grad_picked, precision=lax.Precision.HIGHEST)
    back_one = fetch_weights(joint_weight[0], merge_weight[0], expand_weight[0], shrink_weight[0])
    grad_first, vectors_one, split_one, matrices_one = layer_backward(
        grad_latent, saved_one, gains[0], shifts[0], back_one, segments
    )
    owned_one = reduce_weights(matrices_one)
    embedded_grad = grad_second * (1.0 - occupied)[:, None] + grad_first
    gains_grad, shifts_grad, branch_grad = lax.psum(
        (
            jnp.stack((vectors_one[0], vectors_two[0])),
            jnp.stack((vectors_one[1], vectors_two[1])),
            jnp.stack((vectors_one[2], vectors_two[2])),
        ),
        ("fsdp", "tensor"),
    )
    joint_bias_grad, expand_bias_grad = lax.psum(
        (jnp.stack((split_one[0], split_two[0])), jnp.stack((split_one[1], split_two[1]))), "fsdp"
    )
    joint_grad = jnp.stack((owned_one[0], owned_two[0]))
    merge_grad = jnp.stack((owned_one[1], owned_two[1]))
    expand_grad = jnp.stack((owned_one[2], owned_two[2]))
    shrink_grad = jnp.stack((owned_one[3], owned_two[3]))
    return (
        latent_low,
        language.astype(jnp.bfloat16),
        embedded_grad,
        gains_grad,
        shifts_grad,
        joint_grad,
        joint_bias_grad,
        merge_grad,
        expand_grad,
        expand_bias_grad,
        shrink_grad,
        branch_grad,
    )


def solution(mesh):
    placed = (
        P(("fsdp", "tensor"), None),
        P("fsdp", None),
        P(("fsdp", "tensor"), None),
        P(("fsdp", "tensor"), None),
        P(),
        P(),
        P(None, "fsdp", None, "tensor"),
        P(None, None, "tensor"),
        P(None, "tensor", "fsdp"),
        P(None, "fsdp", "tensor"),
        P(None, "tensor"),
        P(None, "tensor", "fsdp"),
        P(),
    )
    return jax.shard_map(
        shards,
        mesh=mesh,
        in_specs=placed,
        out_specs=(
            P(("fsdp", "tensor"), None),
            P(("fsdp", "tensor"), None),
            P(("fsdp", "tensor"), None),
            P(),
            P(),
            P(None, "fsdp", None, "tensor"),
            P(None, None, "tensor"),
            P(None, "tensor", "fsdp"),
            P(None, "fsdp", "tensor"),
            P(None, "tensor"),
            P(None, "tensor", "fsdp"),
            P(),
        ),
        check_vma=False,
    )
```

profile of v0, /device:TPU:0, one launch (start us, length us, event | category | flops | bytes accessed | tf_op | source)
XLA Modules:
  0.0 1226.3 jit_solution(13794031251392923490)
XLA Ops:
  14.8 12.7 %all_gather.56 = bf16[512,768]{1,0:T(8,128)(2,1)S(1)} all-gather(bf16[256,768]{1,0:T(8,128)(2,1)S(1)} %fusion.111), channel_id=1, replica_groups=mesh['fsdp'=16,'tensor'=2] {'tensor'}, dimensions={0}, use_global_device_ids=true | all-gather | bytes 1179648 | tf_op jit(solution)/shard_map/all_gather | solution.py:21
  27.6 24.0 %all-gather.1 = bf16[1,384,768]{1,2,0:T(8,128)(2,1)S(1)} all-gather(bf16[1,384,48]{1,2,0:T(8,128)(2,1)S(1)} %get-tuple-element.774), channel_id=3, replica_groups=mesh['fsdp'=16,'tensor'=2] {'fsdp'}, dimensions={2}, use_global_device_ids=true | all-gather | bytes 626688 | tf_op jit(solution)/shard_map/all_gather | solution.py:38
  60.5 8.8 while.60
  72.7 15.9 %reduce-scatter.17.cloned.1.call-done = bf16[256,768]{1,0:T(8,128)(2,1)} async-done(((bf16[512,768]{1,0:T(8,128)(2,1)}), bf16[256,768]{1,0:T(8,128)(2,1)}) %reduce-scatter.17.cloned.1.call-update) | async-done | bytes 393232 | tf_op jit(solution)/shard_map/reduce_scatter | solution.py:25
  91.5 11.5 all_gather.59
  103.0 31.0 %all-gather.17.cloned.1.call-done = bf16[1,768,1536]{2,1,0:T(8,128)(2,1)} async-done(((bf16[1,48,1536]{2,1,0:T(8,128)(2,1)}), bf16[1,768,1536]{2,1,0:T(8,128)(2,1)}) %all-gather.17.cloned.1.call-update) | async-done | bytes 2359312 | tf_op jit(solution)/shard_map/all_gather | solution.py:39
  138.8 39.3 %all-gather.19.cloned.1.call-done = bf16[1,1536,768]{1,2,0:T(8,128)(2,1)} async-done(((bf16[1,1536,48]{1,2,0:T(8,128)(2,1)}), bf16[1,1536,768]{1,2,0:T(8,128)(2,1)}) %all-gather.19.cloned.1.call-update) | async-done | bytes 2359312 | tf_op jit(solution)/shard_map/all_gather | solution.py:40
  184.3 20.8 %all-gather.5 = bf16[1,384,768]{1,2,0:T(8,128)(2,1)S(1)} all-gather(bf16[1,384,48]{1,2,0:T(8,128)(2,1)S(1)} %get-tuple-element.773), channel_id=7, replica_groups=mesh['fsdp'=16,'tensor'=2] {'fsdp'}, dimensions={2}, use_global_device_ids=true | all-gather | bytes 626688 | tf_op jit(solution)/shard_map/all_gather | solution.py:38
  207.6 12.6 %all_gather.62 = bf16[512,768]{1,0:T(8,128)(2,1)} all-gather(bf16[256,768]{1,0:T(8,128)(2,1)S(1)} %add_convert_fusion.2), channel_id=1, replica_groups=mesh['fsdp'=16,'tensor'=2] {'tensor'}, dimensions={0}, use_global_device_ids=true | all-gather | bytes 1179648 | tf_op jit(solution)/shard_map/all_gather | solution.py:21
  220.2 22.4 %all-gather.21.cloned.1.call-done = bf16[1,768,3,384]{3,1,2,0:T(8,128)(2,1)} async-done(((bf16[1,48,3,384]{3,1,2,0:T(8,128)(2,1)}), bf16[1,768,3,384]{3,1,2,0:T(8,128)(2,1)}) %all-gather.21.cloned.1.call-update) | async-done | bytes 1769488 | tf_op jit(solution)/shard_map/all_gather | solution.py:37
  251.0 10.7 while.61
  264.8 19.3 %all_gather.68 = bf16[512,768]{1,0:T(8,128)(2,1)} all-gather(bf16[256,768]{1,0:T(8,128)(2,1)S(1)} %copy-done.45), channel_id=1, replica_groups=mesh['fsdp'=16,'tensor'=2] {'tensor'}, dimensions={0}, use_global_device_ids=true | all-gather | bytes 1179648 | tf_op jit(solution)/shard_map/all_gather | solution.py:21
  287.8 11.8 all_gather.65
  299.6 30.3 %all-gather.23.cloned.1.call-done = bf16[1,768,1536]{2,1,0:T(8,128)(2,1)} async-done(((bf16[1,48,1536]{2,1,0:T(8,128)(2,1)}), bf16[1,768,1536]{2,1,0:T(8,128)(2,1)}) %all-gather.23.cloned.1.call-update) | async-done | bytes 2359312 | tf_op jit(solution)/shard_map/all_gather | solution.py:39
  334.7 39.4 %all-gather.25.cloned.1.call-done = bf16[1,1536,768]{1,2,0:T(8,128)(2,1)} async-done(((bf16[1,1536,48]{1,2,0:T(8,128)(2,1)}), bf16[1,1536,768]{1,2,0:T(8,128)(2,1)}) %all-gather.25.cloned.1.call-update) | async-done | bytes 2359312 | tf_op jit(solution)/shard_map/all_gather | solution.py:40
  389.0 10.8 reduce-scatter.25.cloned.1.call-done
  403.8 15.7 %reduce-scatter.23.cloned.1.call-done = bf16[256,768]{1,0:T(8,128)(2,1)} async-done(((bf16[512,768]{1,0:T(8,128)(2,1)}), bf16[256,768]{1,0:T(8,128)(2,1)}) %reduce-scatter.23.cloned.1.call-update) | async-done | bytes 393232 | tf_op jit(solution)/shard_map/reduce_scatter | solution.py:25
  422.3 11.8 all_gather.69
  438.3 44.0 %while.62 = (s32[]{:T(128)}, f32[512,384]{1,0:T(8,128)}, f32[512,384]{0,1:T(8,128)}, f32[2,256,384]{1,2,0:T(8,128)}, s32[2]{0:T(128)S(1)}, /*index=5*/bf16[512,3...) while((s32[]{:T(128)}, f32[512,384]{1,0:T(8,128)}, ...), condition=%wide.region_26.27_spmd, body=%wide.region_24.26_spmd.sunk | while | flops 257560352 | bytes 28270788 | solution.py:130
  489.8 17.5 %reduce-scatter.27.cloned.1.call-done = bf16[256,768]{1,0:T(8,128)(2,1)} async-done(((bf16[512,768]{1,0:T(8,128)(2,1)}), bf16[256,768]{1,0:T(8,128)(2,1)}) %reduce-scatter.27.cloned.1.call-update) | async-done | bytes 393232 | tf_op jit(solution)/shard_map/reduce_scatter | solution.py:25
  511.9 11.5 all_gather.70
  530.7 17.5 %reduce-scatter.29.cloned.1.call-done = bf16[256,768]{1,0:T(8,128)(2,1)} async-done(((bf16[512,768]{1,0:T(8,128)(2,1)}), bf16[256,768]{1,0:T(8,128)(2,1)}) %reduce-scatter.29.cloned.1.call-update) | async-done | bytes 393232 | tf_op jit(solution)/shard_map/reduce_scatter | solution.py:25
  553.5 11.9 all_gather.71
  569.6 44.3 %while.63 = (s32[]{:T(128)}, f32[512,384]{1,0:T(8,128)}, f32[512,384]{0,1:T(8,128)}, f32[2,256,384]{1,2,0:T(8,128)}, s32[2]{0:T(128)S(1)}, /*index=5*/bf16[512,3...) while((s32[]{:T(128)}, f32[512,384]{1,0:T(8,128)}, ...), condition=%wide.region_35.36_spmd, body=%wide.region_33.35_spmd.sunk | while | flops 257560352 | bytes 28270668 | solution.py:130
  674.5 60.4 %all-reduce.1 = (f32[2,2,384]{2,1,0:T(2,128)}, f32[2,1536]{1,0:T(2,128)}) all-reduce(f32[2,2,384]{2,1,0:T(2,128)S(1)} %pad_maximum_fusion.14, f32[2,1536]{1,0:T(2,128)S(1)} %pad_maximum_fusion.12), channel_id=1, replica_groups=mesh['fsdp'=16,'tensor'=2] {'fsdp'}, use_global_device_ids=true, to_apply=%region_55.56 | all-reduce | flops 4608 | bytes 36864 | tf_op jit(solution)/shard_map/psum | solution.py:304
  740.0 38.2 %all-reduce = (f32[2,2,768]{2,1,0:T(2,128)}, f32[2,2,768]{2,1,0:T(2,128)}, f32[2,2,768]{2,1,0:T(2,128)}) all-reduce(f32[2,2,768]{2,1,0:T(2,128)S(1)} %pad_maximum_fusion.10, f32[2,2,768]{2,1,0:T(2,128)S(1)} %pad_maximum_fusion.11, f32[2,2,768]{2,1,0:T(2,128)S(1)} %pad_maximum_fusion.13), channel_id=1, replica_groups=mesh['fsdp'=16,'tensor'=2] {'fsdp','tensor'}, use_global_device_ids=true, to_apply=%region_43.44 | all-reduce | flops 9216 | bytes 73728 | tf_op jit(solution)/shard_map/psum | solution.py:296
  781.2 50.6 %reduce-scatter.35.cloned.1.call-done = f32[48,3,384]{2,0,1:T(8,128)} async-done(((f32[768,3,384]{2,0,1:T(8,128)}), f32[48,3,384]{2,0,1:T(8,128)}) %reduce-scatter.35.cloned.1.call-update) | async-done | bytes 221200 | tf_op jit(solution)/shard_map/reduce_scatter | solution.py:46
  831.7 70.7 %reduce-scatter.33.cloned.1.call-done = f32[48,3,384]{2,0,1:T(8,128)} async-done(((f32[768,3,384]{2,0,1:T(8,128)}), f32[48,3,384]{2,0,1:T(8,128)}) %reduce-scatter.33.cloned.1.call-update) | async-done | bytes 221200 | tf_op jit(solution)/shard_map/reduce_scatter | solution.py:46
  904.3 76.5 %reduce-scatter.47.cloned.1.call-done = f32[1536,48]{0,1:T(8,128)} async-done(((f32[1536,768]{0,1:T(8,128)}), f32[1536,48]{0,1:T(8,128)}) %reduce-scatter.47.cloned.1.call-update) | async-done | bytes 294928 | tf_op jit(solution)/shard_map/reduce_scatter | solution.py:49
  980.7 78.8 %reduce-scatter.45.cloned.1.call-done = f32[1536,48]{0,1:T(8,128)} async-done(((f32[1536,768]{0,1:T(8,128)}), f32[1536,48]{0,1:T(8,128)}) %reduce-scatter.45.cloned.1.call-update) | async-done | bytes 294928 | tf_op jit(solution)/shard_map/reduce_scatter | solution.py:49
  1061.5 76.6 %reduce-scatter.43.cloned.1.call-done = f32[48,1536]{1,0:T(8,128)} async-done(((f32[768,1536]{1,0:T(8,128)}), f32[48,1536]{1,0:T(8,128)}) %reduce-scatter.43.cloned.1.call-update) | async-done | bytes 294928 | tf_op jit(solution)/shard_map/reduce_scatter | solution.py:48
  1138.1 79.0 %reduce-scatter.41.cloned.1.call-done = f32[48,1536]{1,0:T(8,128)} async-done(((f32[768,1536]{1,0:T(8,128)}), f32[48,1536]{1,0:T(8,128)}) %reduce-scatter.41.cloned.1.call-update) | async-done | bytes 294928 | tf_op jit(solution)/shard_map/reduce_scatter | solution.py:48
  (566 shorter events, 278.3 us)
Async XLA Ops:
  7.2 47.7 %all-gather.15.cloned.1.call-start = ((), (), s32[]{:S(2)}) async-start(), calls=%async_computation.32 | async-start | bytes 1880064 | tf_op jit(solution)/shard_map/all_gather | solution.py:37
  8.9 79.7 %reduce-scatter.17.cloned.1.call-start = ((), (), s32[]{:S(2)}) async-start(), calls=%async_computation.16 | async-start | bytes 1179648 | tf_op jit(solution)/shard_map/reduce_scatter | solution.py:25
  70.9 63.1 %all-gather.17.cloned.1.call-start = ((), (), s32[]{:S(2)}) async-start(), calls=%async_computation.33 | async-start | bytes 2506752 | tf_op jit(solution)/shard_map/all_gather | solution.py:39
  71.7 106.3 %all-gather.19.cloned.1.call-start = ((), (), s32[]{:S(2)}) async-start(), calls=%async_computation.34 | async-start | bytes 2506752 | tf_op jit(solution)/shard_map/all_gather | solution.py:40
  72.6 132.6 %reduce-scatter.19.cloned.1.call-start = ((), (), s32[]{:S(2)}) async-start(), calls=%async_computation.17 | async-start | bytes 1179648 | tf_op jit(solution)/shard_map/reduce_scatter | solution.py:25
  183.5 59.1 %all-gather.21.cloned.1.call-start = ((), (), s32[]{:S(2)}) async-start(), calls=%async_computation.35 | async-start | bytes 1880064 | tf_op jit(solution)/shard_map/all_gather | solution.py:37
  184.1 102.1 %reduce-scatter.21.cloned.1.call-start = ((), (), s32[]{:S(2)}) async-start(), calls=%async_computation.18 | async-start | bytes 1179648 | tf_op jit(solution)/shard_map/reduce_scatter | solution.py:25
  207.1 79.1 %copy-start.1 = (f32[256,768]{1,0:T(8,128)}, f32[256,768]{1,0:T(8,128)S(1)}, u32[]{:S(2)}) copy-start(f32[256,768]{1,0:T(8,128)S(1)} %get-tuple-element.776) | copy-start | bytes 2359300
  263.2 66.7 %all-gather.23.cloned.1.call-start = ((), (), s32[]{:S(2)}) async-start(), calls=%async_computation.36 | async-start | bytes 2506752 | tf_op jit(solution)/shard_map/all_gather | solution.py:39
  264.0 110.1 %all-gather.25.cloned.1.call-start = ((), (), s32[]{:S(2)}) async-start(), calls=%async_computation.37 | async-start | bytes 2506752 | tf_op jit(solution)/shard_map/all_gather | solution.py:40
  264.7 135.1 %reduce-scatter.25.cloned.1.call-start = ((), (), s32[]{:S(2)}) async-start(), calls=%async_computation.20 | async-start | bytes 1179648 | tf_op jit(solution)/shard_map/reduce_scatter | solution.py:25
  383.4 36.1 %reduce-scatter.23.cloned.1.call-start = ((), (), s32[]{:S(2)}) async-start(), calls=%async_computation.19 | async-start | bytes 1179648 | tf_op jit(solution)/shard_map/reduce_scatter | solution.py:25
  389.0 118.3 %reduce-scatter.27.cloned.1.call-start = ((), (), s32[]{:S(2)}) async-start(), calls=%async_computation.21 | async-start | bytes 1179648 | tf_op jit(solution)/shard_map/reduce_scatter | solution.py:25
  489.7 58.5 %reduce-scatter.29.cloned.1.call-start = ((), (), s32[]{:S(2)}) async-start(), calls=%async_computation.22 | async-start | bytes 1179648 | tf_op jit(solution)/shard_map/reduce_scatter | solution.py:25
  530.7 205.0 %reduce-scatter.31.cloned.1.call-start = ((), (), s32[]{:S(2)}) async-start(), calls=%async_computation.23 | async-start | bytes 1179648 | tf_op jit(solution)/shard_map/reduce_scatter | solution.py:25
  621.2 158.3 %reduce-scatter.39.cloned.1.call-start = ((), (), s32[]{:S(2)}) async-start(), calls=%async_computation.27 | async-start | bytes 1253376 | tf_op jit(solution)/shard_map/reduce_scatter | solution.py:47
  623.0 156.6 %reduce-scatter.37.cloned.1.call-start = ((), (), s32[]{:S(2)}) async-start(), calls=%async_computation.26 | async-start | bytes 1253376 | tf_op jit(solution)/shard_map/reduce_scatter | solution.py:47
  624.8 207.0 %reduce-scatter.35.cloned.1.call-start = ((), (), s32[]{:S(2)}) async-start(), calls=%async_computation.25 | async-start | bytes 3760128 | tf_op jit(solution)/shard_map/reduce_scatter | solution.py:46
  629.0 273.4 %reduce-scatter.33.cloned.1.call-start = ((), (), s32[]{:S(2)}) async-start(), calls=%async_computation.24 | async-start | bytes 3760128 | tf_op jit(solution)/shard_map/reduce_scatter | solution.py:46
  633.5 347.2 %reduce-scatter.47.cloned.1.call-start = ((), (), s32[]{:S(2)}) async-start(), calls=%async_computation.31 | async-start | bytes 5013504 | tf_op jit(solution)/shard_map/reduce_scatter | solution.py:49
  640.2 419.3 %reduce-scatter.45.cloned.1.call-start = ((), (), s32[]{:S(2)}) async-start(), calls=%async_computation.30 | async-start | bytes 5013504 | tf_op jit(solution)/shard_map/reduce_scatter | solution.py:49
  647.0 491.1 %reduce-scatter.43.cloned.1.call-start = ((), (), s32[]{:S(2)}) async-start(), calls=%async_computation.29 | async-start | bytes 5013504 | tf_op jit(solution)/shard_map/reduce_scatter | solution.py:48
  652.3 564.8 %reduce-scatter.41.cloned.1.call-start = ((), (), s32[]{:S(2)}) async-start(), calls=%async_computation.28 | async-start | bytes 5013504 | tf_op jit(solution)/shard_map/reduce_scatter | solution.py:48
  657.6 78.1 %copy-start.69 = (f32[768]{0:T(1024)S(1)}, f32[768]{0:T(1024)}, u32[]{:S(2)}) copy-start(f32[768]{0:T(1024)} %copy-done.68) | copy-start | bytes 9220
  659.4 118.8 %copy-start.17 = (f32[256,768]{1,0:T(8,128)S(1)}, f32[256,768]{1,0:T(8,128)}, u32[]{:S(2)}) copy-start(f32[256,768]{1,0:T(8,128)} %copy-done.15) | copy-start | bytes 2359300
  659.4 118.8 %copy-start.19 = (f32[256,768]{1,0:T(8,128)S(1)}, f32[256,768]{1,0:T(8,128)}, u32[]{:S(2)}) copy-start(f32[256,768]{1,0:T(8,128)} %copy-done.18) | copy-start | bytes 2359300
  660.1 118.1 %copy-start.21 = (f32[256,768]{1,0:T(8,128)S(1)}, f32[256,768]{1,0:T(8,128)}, u32[]{:S(2)}) copy-start(f32[256,768]{1,0:T(8,128)} %copy-done.20) | copy-start | bytes 2359300
  670.3 69.7 %copy-start.87 = (f32[1,768]{1,0:T(1,128)S(1)}, f32[1,768]{1,0:T(1,128)}, u32[]{:S(2)}) copy-start(f32[1,768]{1,0:T(1,128)} %reshape.631) | copy-start | bytes 9220
  670.3 107.9 %copy-start.72 = (f32[256]{0:T(256)S(1)}, f32[256]{0:T(256)}, u32[]{:S(2)}) copy-start(f32[256]{0:T(256)} %copy-done.71) | copy-start | bytes 3076
  670.3 107.9 %copy-start.78 = (f32[256]{0:T(256)S(1)}, f32[256]{0:T(256)}, u32[]{:S(2)}) copy-start(f32[256]{0:T(256)} %copy-done.77) | copy-start | bytes 3076
  670.3 107.9 %copy-start.89 = (f32[256]{0:T(256)S(1)}, f32[256]{0:T(256)}, u32[]{:S(2)}) copy-start(f32[256]{0:T(256)} %copy-done.88) | copy-start | bytes 3076
  670.3 107.9 %copy-start.96 = (f32[256]{0:T(256)S(1)}, f32[256]{0:T(256)}, u32[]{:S(2)}) copy-start(f32[256]{0:T(256)} %copy-done.95) | copy-start | bytes 3076
  (107 other events, 1391.7 us)
Sparse Core Ops, SparseCore 0:
  10.9 43.9 all-gather.14
  71.0 17.5 reduce-scatter.16
  91.8 42.2 all-gather.16
  137.0 40.9 all-gather.18
  183.7 16.2 reduce-scatter.18
  202.1 40.4 all-gather.20
  263.3 22.8 reduce-scatter.20
  288.7 41.1 all-gather.22
  333.1 40.9 all-gather.24
  383.5 16.2 reduce-scatter.24
  402.0 17.4 reduce-scatter.22
  489.8 17.4 reduce-scatter.26
  530.8 17.4 reduce-scatter.28
  621.3 17.4 reduce-scatter.30
  642.3 58.0 reduce-scatter.38
  703.8 57.1 reduce-scatter.36
  764.7 66.9 reduce-scatter.34
  835.5 66.9 reduce-scatter.32
  906.3 74.4 reduce-scatter.46
  984.9 74.5 reduce-scatter.44
  1063.4 74.6 reduce-scatter.42
  1142.5 74.5 reduce-scatter.40
where the time goes:
time: 1240 us; the launch traced here: 1230 us
  waiting for transfers between devices  680 us (55%)
  blocking collectives  247 us (20%)
  matrix products  123 us (10%)
  local copies, waits for them, and re-layouts  88.3 us (7%)
  other arithmetic  58.2 us (5%)
  between operations  16 us (1%)
  loops' own time  13.3 us (1%)
    reduce_scatter x2, waiting for transfers between devices, reduce_weights(): lax.psum_scatter(matrices[2], 'fsdp', scatter_dimension=0, tiled=True)  156 us
    reduce_scatter x2, waiting for transfers between devices, reduce_weights(): lax.psum_scatter(matrices[3], 'fsdp', scatter_dimension=1, tiled=True)  155 us
    reduce_scatter x2, waiting for transfers between devices, reduce_weights(): lax.psum_scatter(matrices[0], 'fsdp', scatter_dimension=0, tiled=True)  121 us
    all_gather x8, blocking collectives, gather_rows(): return lax.all_gather(rows, 'tensor', axis=0, tiled=True)  103 us
    reduce_scatter x8, waiting for transfers between devices, scatter_rows(): lax.psum_scatter(jnp.einsum(pattern, source, weight, preferred_element_ty...  79.6 us
    all_gather x2, waiting for transfers between devices, fetch_weights(): lax.all_gather(shrink, 'fsdp', axis=1, tiled=True)  78.6 us
    all_gather x2, waiting for transfers between devices, fetch_weights(): lax.all_gather(expand, 'fsdp', axis=0, tiled=True)  61.4 us
    psum x1, blocking collectives, shards(): lax.psum((jnp.stack((split_one[0], split_two[0])), jnp.stack((split_one[1...  60.4 us
  transfers between devices with their start and end apart: 22, of which 18 were waited for; matrix products, arithmetic and copies ran while one was open for 7% of the time, Pallas kernels for 0%

commit v1 on v0

v1 whole, which is shorter than its diff:
```python
from functools import partial

import jax
import jax.numpy as jnp
from jax import lax
from jax.experimental import pallas as pl
from jax.experimental.pallas import tpu as pltpu
from jax.sharding import PartitionSpec as P

HEAD = 64
LANES = 128
EPSILON = 1e-05
BF = jnp.bfloat16
F32 = jnp.float32
GELU_C = 0.7978845608028654
GELU_A = 0.044715
MIB = 1 << 20


def dot(a, b):
    return lax.dot_general(a, b, (((1,), (0,)), ((), ())), preferred_element_type=F32)


def dot_nt(a, b):
    return lax.dot_general(a, b, (((1,), (1,)), ((), ())), preferred_element_type=F32)


def dot_tn(a, b):
    return lax.dot_general(a, b, (((0,), (0,)), ((), ())), preferred_element_type=F32)


def factors_of(count):
    found = []
    if count % 2 == 0:
        found.append(2)
        count //= 2
    if count % 2 == 0 and (count.bit_length() - 1) % 2 == 1:
        found.append(2)
        count //= 2
    while count > 1:
        step = 4 if count % 4 == 0 else 2 if count % 2 == 0 else count
        found.append(step)
        count //= step
    return found


def shift_pairs(count, stride, size, by):
    pairs = []
    for source in range(count):
        place = (source // stride) % size
        target = source + ((place + by) % size - place) * stride
        pairs.append((source, target))
    return pairs


def swap(value):
    return lax.ppermute(value, "tensor", [(0, 1), (1, 0)])


def gather_shards(shard, count):
    me = lax.axis_index("fsdp")
    index = jnp.arange(count)
    place = jnp.zeros((count,), jnp.int32)
    sizes = factors_of(count)
    strides = [1]
    for size in sizes:
        strides.append(strides[-1] * size)
    held = shard[None]
    for size, stride in reversed(list(zip(sizes, strides))):
        width = held.shape[0]
        parts = [held]
        for by in range(1, size):
            parts.append(lax.ppermute(held, "fsdp", shift_pairs(count, stride, size, by)))
        held = jnp.concatenate(parts, axis=0)
        mine = (me // stride) % size
        theirs = (index // stride) % size
        place = place + ((mine - theirs) % size) * width
    return (held, place)


def unpack_kernel(place_ref, held_ref, *outs):
    del place_ref
    first = 0
    for out in outs:
        if out.ndim == 3:
            rows = out.shape[1]
            out[...] = held_ref[:, first : first + rows, :]
            first += rows
        else:
            rows = out.shape[2]
            for one in range(out.shape[0]):
                out[one] = held_ref[:, first : first + rows, :]
                first += rows


def unpack(held, place, kinds):
    count, rows, width = held.shape
    each = rows // sum(max(kind, 1) for kind in kinds)
    shapes, specs = [], []
    for kind in kinds:
        if kind:
            shapes.append(jax.ShapeDtypeStruct((kind, count, each, width), held.dtype))
            specs.append(pl.BlockSpec((kind, 1, each, width), lambda i, p: (0, i, 0, 0)))
        else:
            shapes.append(jax.ShapeDtypeStruct((count, each, width), held.dtype))
            specs.append(pl.BlockSpec((1, each, width), lambda i, p: (i, 0, 0)))
    outs = pl.pallas_call(
        unpack_kernel,
        name="unpack",
        out_shape=shapes,
        grid_spec=pltpu.PrefetchScalarGridSpec(
            num_scalar_prefetch=1,
            grid=(count,),
            in_specs=[pl.BlockSpec((1, rows, width), lambda i, p: (p[i], 0, 0))],
            out_specs=specs,
        ),
        compiler_params=pltpu.CompilerParams(vmem_limit_bytes=16 * MIB),
        cost_estimate=pl.CostEstimate(
            flops=0, transcendentals=0, bytes_accessed=4 * count * rows * width
        ),
    )(place, held)
    return [
        out.reshape(out.shape[:-3] + (out.shape[-3] * out.shape[-2], width)) for out in outs
    ]


def reduce_shards(blocks, count):
    me = lax.axis_index("fsdp")
    held = blocks
    stride = 1
    for size in factors_of(count):
        mine = (me // stride) % size
        split = held.reshape((held.shape[0] // size, size) + held.shape[1:])
        total = lax.dynamic_index_in_dim(split, mine, 1, keepdims=False).astype(F32)
        for by in range(1, size):
            sent = lax.dynamic_index_in_dim(split, (mine + by) % size, 1, keepdims=False)
            got = lax.ppermute(
                sent.astype(BF), "fsdp", shift_pairs(count, stride, size, by)
            )
            total = total + got.astype(F32)
        held = total
        stride *= size
    return held[0]


def sum_everywhere(value, count):
    stride = 1
    while stride < count and count % (2 * stride) == 0:
        pairs = [(source, source ^ stride) for source in range(count)]
        value = value + lax.ppermute(value, "fsdp", pairs)
        stride *= 2
    if stride < count:
        groups = [list(range(first, count, stride)) for first in range(stride)]
        value = lax.psum(value, "fsdp", axis_index_groups=groups)
    return value


def lane_masks(rows):
    lane = lax.broadcasted_iota(jnp.int32, (rows, LANES), 1)
    return (lane < HEAD, lane >= HEAD)


def attend_forward_kernel(
    n_ref, wj_ref, wm_ref, bias_ref, seg_col_ref, seg_row_ref,
    part_ref, q_ref, k_ref, v_ref, mixed_ref, neg_ref,
):
    seq = n_ref.shape[0]
    half = seq // 2
    n = n_ref[...]
    q_ref[...] = (dot(n, wj_ref[0]) + bias_ref[0:1, :]).astype(BF)
    k_ref[...] = dot(n, wj_ref[1]).astype(BF)
    v_ref[...] = (dot(n, wj_ref[2]) + bias_ref[1:2, :]).astype(BF)
    rows = lax.broadcasted_iota(jnp.int32, (seq, seq), 0)
    cols = lax.broadcasted_iota(jnp.int32, (seq, seq), 1)
    allowed = (seg_col_ref[...] == seg_row_ref[...]) & (cols <= rows)
    neg_ref[...] = jnp.where(allowed, 0.0, -1e30)
    masks = lane_masks(half)
    for pair in range(q_ref.shape[1] // LANES):
        lanes = slice(pair * LANES, (pair + 1) * LANES)
        for part in range(2):
            top = slice(part * half, (part + 1) * half)
            keys = slice(0, (part + 1) * half)
            qp = q_ref[top, lanes] * BF(HEAD ** (-0.5))
            kp = k_ref[keys, lanes]
            vp = v_ref[keys, lanes]
            found = []
            for mask in masks:
                s = dot_nt(jnp.where(mask, qp, BF(0)), kp) + neg_ref[top, keys]
                e = jnp.exp(s - jnp.max(s, axis=-1, keepdims=True))
                scale = 1.0 / jnp.sum(e, axis=-1, keepdims=True)
                found.append(dot((e * scale).astype(BF), vp))
            mixed_ref[top, lanes] = jnp.where(masks[0], found[0], found[1]).astype(BF)
    part_ref[...] = dot_nt(mixed_ref[...], wm_ref[...]).astype(BF)


def attend_forward(n, wj, wm, bias, segments):
    seq, d = n.shape
    width = wm.shape[1]
    rows = jax.ShapeDtypeStruct((seq, width), BF)
    flops = 2 * seq * d * width * 4 + 4 * seq * seq * width
    return pl.pallas_call(
        attend_forward_kernel,
        name="attend_forward",
        out_shape=[jax.ShapeDtypeStruct((seq, d), BF), rows, rows, rows, rows],
        scratch_shapes=[pltpu.VMEM((seq, seq), F32)],
        compiler_params=pltpu.CompilerParams(vmem_limit_bytes=24 * MIB),
        cost_estimate=pl.CostEstimate(
            flops=flops,
            transcendentals=seq * seq * width // HEAD,
            bytes_accessed=2 * (4 * d * width + 2 * seq * d + 4 * seq * width),
        ),
    )(n, wj, wm, bias, segments.reshape(seq, 1), segments.reshape(1, seq))


def attend_backward_kernel(
    n_ref, q_ref, k_ref, v_ref, mixed_ref, gm_ref, wj_ref, wm_ref, seg_col_ref, seg_row_ref,
    gn_ref, gj_ref, gw_ref, gb_ref, dj_ref, neg_ref, gx_ref,
):
    count, seq, _ = n_ref.shape
    width = q_ref.shape[2]
    half = seq // 2
    masks = lane_masks(half)
    rows = lax.broadcasted_iota(jnp.int32, (seq, seq), 0)
    cols = lax.broadcasted_iota(jnp.int32, (seq, seq), 1)
    for one in range(count):
        gx_ref[...] = dot(gm_ref[one], wm_ref[...]).astype(BF)
        allowed = (seg_col_ref[one] == seg_row_ref[one]) & (cols <= rows)
        neg_ref[...] = jnp.where(allowed, 0.0, -1e30)
        sums = [[], []]
        for pair in range(width // LANES):
            lanes = slice(pair * LANES, (pair + 1) * LANES)
            dk = [None, None]
            dv = [None, None]
            dq_all = []
            for part in range(2):
                top = slice(part * half, (part + 1) * half)
                keys = slice(0, (part + 1) * half)
                qp = q_ref[one, top, lanes]
                kp = k_ref[one, keys, lanes]
                vp = v_ref[one, keys, lanes]
                gp = gx_ref[top, lanes]
                dq, dk_now, dv_now = [], [], []
                for mask in masks:
                    qm = jnp.where(mask, qp, BF(0)) * BF(HEAD ** (-0.5))
                    s = dot_nt(qm, kp) + neg_ref[top, keys]
                    e = jnp.exp(s - jnp.max(s, axis=-1, keepdims=True))
                    p = e * (1.0 / jnp.sum(e, axis=-1, keepdims=True))
                    gprobs = dot_nt(jnp.where(mask, gp, BF(0)), vp)
                    inner = jnp.sum(gprobs * p, axis=-1, keepdims=True)
                    ds = (p * (gprobs - inner) * HEAD ** (-0.5)).astype(BF)
                    dq.append(dot(ds, kp))
                    dk_now.append(dot_tn(ds, qp))
                    dv_now.append(dot_tn(p.astype(BF), gp))
                dq_all.append(jnp.where(masks[0], dq[0], dq[1]))
                for block in range(part + 1):
                    at = slice(block * half, (block + 1) * half)
                    k_new = jnp.where(masks[0], dk_now[0][at], dk_now[1][at])
                    v_new = jnp.where(masks[0], dv_now[0][at], dv_now[1][at])
                    dk[block] = k_new if dk[block] is None else dk[block] + k_new
                    dv[block] = v_new if dv[block] is None else dv[block] + v_new
            sums[0].append(
                jnp.sum(dq_all[0], axis=0, keepdims=True)
                + jnp.sum(dq_all[1], axis=0, keepdims=True)
            )
            sums[1].append(
                jnp.sum(dv[0], axis=0, keepdims=True) + jnp.sum(dv[1], axis=0, keepdims=True)
            )
            for part in range(2):
                at = slice(part * half, (part + 1) * half)
                dj_ref[0, one, at, lanes] = dq_all[part].astype(BF)
                dj_ref[1, one, at, lanes] = dk[part].astype(BF)
                dj_ref[2, one, at, lanes] = dv[part].astype(BF)
        for which in range(2):
            total = jnp.concatenate(sums[which], axis=1)
            if one == 0:
                gb_ref[which : which + 1, :] = total
            else:
                gb_ref[which : which + 1, :] = gb_ref[which : which + 1, :] + total
        gn = dot_nt(dj_ref[0, one], wj_ref[0])
        gn = gn + dot_nt(dj_ref[1, one], wj_ref[1])
        gn = gn + dot_nt(dj_ref[2, one], wj_ref[2])
        gn_ref[one] = gn.astype(BF)
    d = n_ref.shape[2]
    nt = n_ref[...].reshape(count * seq, d).T
    for which in range(3):
        gj_ref[which] = dot(nt, dj_ref[which].reshape(count * seq, width)).astype(BF)
    gmt = gm_ref[...].reshape(count * seq, d).T
    gw_ref[...] = dot(gmt, mixed_ref[...].reshape(count * seq, width)).astype(BF)


def attend_backward(n, q, k, v, mixed, gm, wj, wm, segments):
    count, seq, d = n.shape
    width = wm.shape[1]
    flops = count * (2 * seq * d * width * 8 + 10 * seq * seq * width)
    return pl.pallas_call(
        attend_backward_kernel,
        name="attend_backward",
        out_shape=[
            jax.ShapeDtypeStruct((count, seq, d), BF),
            jax.ShapeDtypeStruct((3, d, width), BF),
            jax.ShapeDtypeStruct((d, width), BF),
            jax.ShapeDtypeStruct((2, width), F32),
        ],
        scratch_shapes=[
            pltpu.VMEM((3, count, seq, width), BF),
            pltpu.VMEM((seq, seq), F32),
            pltpu.VMEM((seq, width), BF),
        ],
        compiler_params=pltpu.CompilerParams(vmem_limit_bytes=40 * MIB),
        cost_estimate=pl.CostEstimate(
            flops=flops,
            transcendentals=count * seq * seq * width // HEAD,
            bytes_accessed=2 * (8 * d * width + count * (3 * seq * d + 4 * seq * width)),
        ),
    )(n, q, k, v, mixed, gm, wj, wm, segments[:, :, None], segments[:, None, :])


def mlp_forward_kernel(n_ref, we_ref, ws_ref, be_ref, out_ref, acc_ref):
    step = pl.program_id(0)
    u = dot(n_ref[...], we_ref[...]) + be_ref[...]
    t = jnp.tanh(GELU_C * (u + GELU_A * (u * u * u)))
    active = (0.5 * u * (1.0 + t)).astype(BF)
    more = dot_nt(active, ws_ref[...])

    @pl.when(step == 0)
    def _():
        acc_ref[...] = more

    @pl.when(step > 0)
    def _():
        acc_ref[...] = acc_ref[...] + more

    @pl.when(step == pl.num_programs(0) - 1)
    def _():
        out_ref[...] = acc_ref[...].astype(BF)


def mlp_forward(n, we, ws, be):
    rows, d = n.shape
    hidden = we.shape[1]
    block = 512 if hidden % 512 == 0 else hidden
    return pl.pallas_call(
        mlp_forward_kernel,
        name="mlp_forward",
        out_shape=jax.ShapeDtypeStruct((rows, d), BF),
        grid=(hidden // block,),
        in_specs=[
            pl.BlockSpec((rows, d), lambda i: (0, 0)),
            pl.BlockSpec((d, block), lambda i: (0, i)),
            pl.BlockSpec((d, block), lambda i: (0, i)),
            pl.BlockSpec((1, block), lambda i: (0, i)),
        ],
        out_specs=pl.BlockSpec((rows, d), lambda i: (0, 0)),
        scratch_shapes=[pltpu.VMEM((rows, d), F32)],
        compiler_params=pltpu.CompilerParams(vmem_limit_bytes=24 * MIB),
        cost_estimate=pl.CostEstimate(
            flops=4 * rows * d * hidden,
            transcendentals=rows * hidden,
            bytes_accessed=4 * d * hidden + 4 * rows * d,
        ),
    )(n, we, ws, be.reshape(1, hidden))


def mlp_backward_kernel(
    n_ref, g_ref, we_ref, ws_ref, be_ref,
    out_ref, gn_ref, ge_ref, gs_ref, gb_ref, acc_ref, gacc_ref, nt_ref, gt_ref,
):
    step = pl.program_id(0)

    @pl.when(step == 0)
    def _():
        nt_ref[...] = n_ref[...].T
        gt_ref[...] = g_ref[...].T

    u = dot(n_ref[...], we_ref[...]) + be_ref[...]
    square = u * u
    t = jnp.tanh(GELU_C * (u + GELU_A * (square * u)))
    lean = 0.5 * (1.0 + t)
    active = (u * lean).astype(BF)
    slope = lean + (0.5 * u) * (1.0 - t * t) * (GELU_C + (3.0 * GELU_C * GELU_A) * square)
    gh = dot(g_ref[...], ws_ref[...]) * slope
    gb_ref[...] = jnp.sum(gh, axis=0, keepdims=True)
    gh = gh.astype(BF)
    gs_ref[...] = dot(gt_ref[...], active).astype(BF)
    ge_ref[...] = dot(nt_ref[...], gh).astype(BF)
    more = dot_nt(active, ws_ref[...])
    gmore = dot_nt(gh, we_ref[...])

    @pl.when(step == 0)
    def _():
        acc_ref[...] = more
        gacc_ref[...] = gmore

    @pl.when(step > 0)
    def _():
        acc_ref[...] = acc_ref[...] + more
        gacc_ref[...] = gacc_ref[...] + gmore

    @pl.when(step == pl.num_programs(0) - 1)
    def _():
        out_ref[...] = acc_ref[...].astype(BF)
        gn_ref[...] = gacc_ref[...].astype(BF)


def mlp_backward(n, g, we, ws, be):
    rows, d = n.shape
    hidden = we.shape[1]
    block = 512 if hidden % 512 == 0 else hidden
    return pl.pallas_call(
        mlp_backward_kernel,
        name="mlp_backward",
        out_shape=[
            jax.ShapeDtypeStruct((rows, d), BF),
            jax.ShapeDtypeStruct((rows, d), BF),
            jax.ShapeDtypeStruct((d, hidden), BF),
            jax.ShapeDtypeStruct((d, hidden), BF),
            jax.ShapeDtypeStruct((1, hidden), F32),
        ],
        grid=(hidden // block,),
        in_specs=[
            pl.BlockSpec((rows, d), lambda i: (0, 0)),
            pl.BlockSpec((rows, d), lambda i: (0, 0)),
            pl.BlockSpec((d, block), lambda i: (0, i)),
            pl.BlockSpec((d, block), lambda i: (0, i)),
            pl.BlockSpec((1, block), lambda i: (0, i)),
        ],
        out_specs=[
            pl.BlockSpec((rows, d), lambda i: (0, 0)),
            pl.BlockSpec((rows, d), lambda i: (0, 0)),
            pl.BlockSpec((d, block), lambda i: (0, i)),
            pl.BlockSpec((d, block), lambda i: (0, i)),
            pl.BlockSpec((1, block), lambda i: (0, i)),
        ],
        scratch_shapes=[
            pltpu.VMEM((rows, d), F32),
            pltpu.VMEM((rows, d), F32),
            pltpu.VMEM((d, rows), BF),
            pltpu.VMEM((d, rows), BF),
        ],
        compiler_params=pltpu.CompilerParams(vmem_limit_bytes=40 * MIB),
        cost_estimate=pl.CostEstimate(
            flops=12 * rows * d * hidden,
            transcendentals=rows * hidden,
            bytes_accessed=8 * d * hidden + 8 * rows * d,
        ),
    )(n, g, we, ws, be.reshape(1, hidden))


def statistics(rows):
    mean = jnp.mean(rows, axis=-1, keepdims=True)
    center = rows - mean
    scale = lax.rsqrt(jnp.mean(center * center, axis=-1, keepdims=True) + EPSILON)
    return (center, scale)


def layer_norm(rows, gain, shift):
    center, scale = statistics(rows)
    return (center * scale * gain + shift).astype(BF)


def layer_norm_backward(rows, grad, gain):
    center, scale = statistics(rows)
    unit = center * scale
    e = grad * gain
    back = scale * (
        e
        - jnp.mean(e, axis=-1, keepdims=True)
        - unit * jnp.mean(e * unit, axis=-1, keepdims=True)
    )
    return (back, jnp.sum(grad * unit, axis=0), jnp.sum(grad, axis=0))


def exact_dot(a, b):
    return jnp.dot(a, b, precision=lax.Precision.HIGHEST, preferred_element_type=F32)


def own_first(value, mine):
    return jnp.stack(
        (
            lax.dynamic_index_in_dim(value, mine, 0, keepdims=False),
            lax.dynamic_index_in_dim(value, 1 - mine, 0, keepdims=False),
        )
    )


def shards(
    count,
    embedded,
    segments,
    thoughts,
    cotangent,
    norm_gains,
    norm_shifts,
    joint_weight,
    joint_bias,
    merge_weight,
    expand_weight,
    expand_bias,
    shrink_weight,
    branch_biases,
):
    mine = lax.axis_index("tensor")
    gains = norm_gains.astype(F32)
    shifts = norm_shifts.astype(F32)
    pair_bias = joint_bias.astype(F32)
    expand_shift = expand_bias.astype(F32)
    biases = branch_biases.astype(F32)
    seq, d = embedded.shape
    rows_each = joint_weight.shape[1]
    width = joint_weight.shape[3]
    hidden = expand_weight.shape[2]

    def attend_pack(layer):
        return jnp.concatenate(
            (
                joint_weight[layer].transpose(1, 0, 2).reshape(3 * rows_each, width),
                merge_weight[layer].T,
            ),
            axis=0,
        )

    def mlp_pack(layer):
        return jnp.concatenate((expand_weight[layer], shrink_weight[layer].T), axis=0)

    attend_weights, mlp_weights = [], []
    for layer in range(2):
        held, place = gather_shards(attend_pack(layer), count)
        attend_weights.append(unpack(held, place, (3, 0)))
        held, place = gather_shards(mlp_pack(layer), count)
        mlp_weights.append(unpack(held, place, (0, 0)))

    segs = own_first(segments, mine)
    places = jnp.arange(seq)
    slots = thoughts[0]
    slots_peer = swap(thoughts)[0]
    slot_cols = (places[:, None] == slots[None, :]).astype(F32)
    source_cols = (places[:, None] == (slots - 1)[None, :]).astype(F32)
    source_peer = (places[:, None] == (slots_peer - 1)[None, :]).astype(BF)
    known = (slots >= 1)[:, None]
    occupied = jnp.sum(slot_cols, axis=1)[:, None]
    cot_peer = swap(cotangent)

    def attention(layer, own):
        peer = swap(own)
        wj, wm = attend_weights[layer]
        peer_part, *peer_kept = attend_forward(peer, wj, wm, pair_bias[layer], segs[1])
        got = swap(peer_part)
        own_part, *own_kept = attend_forward(own, wj, wm, pair_bias[layer], segs[0])
        kept = [jnp.stack(both) for both in zip([own] + own_kept, [peer] + peer_kept)]
        return (own_part.astype(F32) + got.astype(F32), kept)

    first = embedded.astype(F32)
    normed = layer_norm(first, gains[0, 0], shifts[0, 0])
    part, kept_one = attention(0, normed)
    middle_one = first + part + biases[0, 0]
    n2_one = layer_norm(middle_one, gains[0, 1], shifts[0, 1])

    slot_count = slots.shape[0]
    pick = source_cols.T
    n2_picked = exact_dot(pick, n2_one.astype(F32)).astype(BF)
    middle_picked = exact_dot(pick, middle_one)
    n2_pair = jnp.concatenate((n2_picked, swap(n2_picked)), axis=0)
    we, ws = mlp_weights[0]
    out = mlp_forward(n2_pair, we, ws, expand_shift[0])
    latent_picked = (
        middle_picked
        + out[:slot_count].astype(F32)
        + swap(out[slot_count:]).astype(F32)
        + biases[0, 1]
    ).astype(BF)
    latent_picked = jnp.where(known, latent_picked, BF(0))
    second = first * (1.0 - occupied) + jnp.dot(
        slot_cols.astype(BF), latent_picked, preferred_element_type=F32
    )

    normed = layer_norm(second, gains[1, 0], shifts[1, 0])
    part, kept_two = attention(1, normed)
    middle_two = second + part + biases[1, 0]
    n2_two = layer_norm(middle_two, gains[1, 1], shifts[1, 1])
    n2_all = jnp.concatenate((n2_two, swap(n2_two)), axis=0)
    g_all = jnp.concatenate((cotangent, cot_peer), axis=0)
    we, ws = mlp_weights[1]
    out, gn, ge_two, gs_two, gb_two = mlp_backward(n2_all, g_all, we, ws, expand_shift[1])
    got = swap(gn[seq:])
    language = middle_two + out[:seq].astype(F32) + swap(out[seq:]).astype(F32) + biases[1, 1]

    def rows_of(array):
        return array.reshape((count, rows_each) + array.shape[1:])

    def reduce_mlp(ge, gs):
        done = reduce_shards(jnp.concatenate((rows_of(ge), rows_of(gs)), axis=1), count)
        return (done[:rows_each], done[rows_each:])

    def reduce_attend(gj, gw):
        done = reduce_shards(
            jnp.concatenate([rows_of(one) for one in (gj[0], gj[1], gj[2], gw)], axis=1), count
        ).reshape(4, rows_each, width)
        return (done[:3], done[3])

    expand_two, shrink_two = reduce_mlp(ge_two, gs_two)

    cot = cotangent.astype(F32)
    back, gain_22, shift_22 = layer_norm_backward(
        middle_two, gn[:seq].astype(F32) + got.astype(F32), gains[1, 1]
    )
    grad_middle = cot + back
    gm = grad_middle.astype(BF)

    def attention_back(layer, gm_pair, kept):
        wj, wm = attend_weights[layer]
        gn, gj, gw, gb = attend_backward(*kept, gm_pair, wj, wm, segs)
        return (gn[0].astype(F32) + swap(gn[1]).astype(F32), gj, gw, gb)

    grad_normed, gj_two, gw_two, pair_two = attention_back(
        1, jnp.stack((gm, swap(gm))), kept_two
    )
    joint_two, merge_two = reduce_attend(gj_two, gw_two)
    back, gain_21, shift_21 = layer_norm_backward(second, grad_normed, gains[1, 0])
    grad_second = grad_middle + back

    g_picked = jnp.where(known, exact_dot(slot_cols.T, grad_second), 0.0)
    g_low = g_picked.astype(BF)
    g_pair = jnp.concatenate((g_low, swap(g_low)), axis=0)
    we, ws = mlp_weights[0]
    _, gn, ge_one, gs_one, gb_one = mlp_backward(n2_pair, g_pair, we, ws, expand_shift[0])
    grad_n2 = gn[:slot_count].astype(F32) + swap(gn[slot_count:]).astype(F32)
    expand_one, shrink_one = reduce_mlp(ge_one, gs_one)
    back, gain_12, shift_12 = layer_norm_backward(middle_picked, grad_n2, gains[0, 1])
    gm_picked = g_picked + back
    gm_low = gm_picked.astype(BF)
    gm_own = jnp.dot(source_cols.astype(BF), gm_low, preferred_element_type=F32).astype(BF)
    gm_peer = jnp.dot(source_peer, swap(gm_low), preferred_element_type=F32).astype(BF)
    grad_normed, gj_one, gw_one, pair_one = attention_back(
        0, jnp.stack((gm_own, gm_peer)), kept_one
    )
    joint_one, merge_one = reduce_attend(gj_one, gw_one)
    back, gain_11, shift_11 = layer_norm_backward(first, grad_normed, gains[0, 0])
    grad_first = exact_dot(source_cols, gm_picked) + back
    embedded_grad = grad_second * (1.0 - occupied) + grad_first

    n2_all = jnp.concatenate((n2_one, swap(n2_one)), axis=0)
    we, ws = mlp_weights[0]
    out = mlp_forward(n2_all, we, ws, expand_shift[0])
    latent = middle_one + out[:seq].astype(F32) + swap(out[seq:]).astype(F32) + biases[0, 1]

    vectors = jnp.stack(
        (
            gain_11, gain_12, gain_21, gain_22,
            shift_11, shift_12, shift_21, shift_22,
            jnp.sum(gm_picked, axis=0), jnp.sum(g_picked, axis=0),
            jnp.sum(grad_middle, axis=0), jnp.sum(cot, axis=0),
        )
    ).reshape(-1)
    vectors = vectors + swap(vectors)
    halves = jnp.concatenate(
        (pair_one.reshape(-1), pair_two.reshape(-1), gb_one.reshape(-1), gb_two.reshape(-1))
    )
    total = sum_everywhere(jnp.concatenate((vectors, halves)), count)
    gains_grad = total[: 4 * d].reshape(2, 2, d)
    shifts_grad = total[4 * d : 8 * d].reshape(2, 2, d)
    branch_grad = total[8 * d : 12 * d].reshape(2, 2, d)
    joint_bias_grad = total[12 * d : 12 * d + 4 * width].reshape(2, 2, width)
    expand_bias_grad = total[12 * d + 4 * width :].reshape(2, hidden)

    return (
        latent.astype(BF),
        language.astype(BF),
        embedded_grad,
        gains_grad,
        shifts_grad,
        jnp.stack((joint_one, joint_two)).transpose(0, 2, 1, 3),
        joint_bias_grad,
        jnp.stack((merge_one, merge_two)).transpose(0, 2, 1),
        jnp.stack((expand_one, expand_two)),
        expand_bias_grad,
        jnp.stack((shrink_one, shrink_two)).transpose(0, 2, 1),
        branch_grad,
    )


def solution(mesh):
    placed = (
        P(("fsdp", "tensor"), None),
        P("fsdp", None),
        P(("fsdp", "tensor"), None),
        P(("fsdp", "tensor"), None),
        P(),
        P(),
        P(None, "fsdp", None, "tensor"),
        P(None, None, "tensor"),
        P(None, "tensor", "fsdp"),
        P(None, "fsdp", "tensor"),
        P(None, "tensor"),
        P(None, "tensor", "fsdp"),
        P(),
    )
    return jax.shard_map(
        partial(shards, mesh.shape["fsdp"]),
        mesh=mesh,
        in_specs=placed,
        out_specs=(
            P(("fsdp", "tensor"), None),
            P(("fsdp", "tensor"), None),
            P(("fsdp", "tensor"), None),
            P(),
            P(),
            P(None, "fsdp", None, "tensor"),
            P(None, None, "tensor"),
            P(None, "tensor", "fsdp"),
            P(None, "fsdp", "tensor"),
            P(None, "tensor"),
            P(None, "tensor", "fsdp"),
            P(),
        ),
        check_vma=False,
    )
```

time: 1240 us -> 493 us (0.40)
  the two profiles are of different devices: /device:TPU:0 before, /device:TPU:24 now
where the time goes in v1:
time: 493 us; the launch traced here: 486 us
  waiting for transfers between devices  220 us (45%)
  Pallas kernels  72.7 us (15%)
  starting transfers between devices  71.9 us (15%)
  other arithmetic  60.8 us (12%)
  local copies, waits for them, and re-layouts  51.5 us (10%)
  matrix products  6.88 us (1%)
    ppermute x20, waiting for transfers between devices, swap(): return lax.ppermute(value, 'tensor', [(0, 1), (1, 0)])  74.5 us
    ppermute x20, waiting for transfers between devices, reduce_shards(): lax.ppermute(sent.astype(BF), 'fsdp', shift_pairs(count, stride, size, by))  73.8 us
    ppermute x20, waiting for transfers between devices, gather_shards(): lax.ppermute(held, 'fsdp', shift_pairs(count, stride, size, by))  67.9 us
    pallas_call x2, Pallas kernels, attend_backward(): pl.pallas_call(attend_backward_kernel, name='attend_backward', out_shape=...  30 us
    unnamed x185, local copies, waits for them, and re-layouts  25.5 us
    ppermute x20, starting transfers between devices, reduce_shards(): lax.ppermute(sent.astype(BF), 'fsdp', shift_pairs(count, stride, size, by))  24.1 us
    ppermute x20, starting transfers between devices, gather_shards(): lax.ppermute(held, 'fsdp', shift_pairs(count, stride, size, by))  22.7 us
    ppermute x20, starting transfers between devices, swap(): return lax.ppermute(value, 'tensor', [(0, 1), (1, 0)])  20.7 us
  transfers between devices with their start and end apart: 64, of which 34 were waited for; matrix products, arithmetic and copies ran while one was open for 20% of the time, Pallas kernels for 12%

profile of v1, /device:TPU:24, one launch (start us, length us, event | category | flops | bytes accessed | tf_op | source)
XLA Modules:
  0.0 486.4 jit_solution(3735131961356645409)
XLA Ops:
  35.9 9.2 %collective-permute-done.17 = bf16[1,192,384]{2,1,0:T(8,128)(2,1)} collective-permute-done((bf16[1,192,384]{2,1,0:T(8,128)(2,1)}, bf16[1,192,384]{2,1,0:T(8,128)(2,1)}, u32[]{:S(2)}, u32[]{:S(2)}) %collective-permute-start.17) | collective-permute-done | bytes 147488 | tf_op jit(solution)/shard_map/ppermute | solution.py:73
  60.6 6.3 %collective-permute-start.9 = (bf16[1,96,1536]{2,1,0:T(8,128)(2,1)S(1)}, bf16[1,96,1536]{2,1,0:T(8,128)(2,1)S(1)}, u32[]{:S(2)}, u32[]{:S(2)}) collective-permute-start(bf16[1,96,1536]{2,1,0:T(8,128)(2,1)S(1)} %copy-done.59), channel_id=1, source_target_pairs={{0,16},{2,18},{4,20},{6,22},{8,24},{10,26},{12,28},{14,30},{16,0},... | collective-permute-start | bytes 884744 | tf_op jit(solution)/shard_map/ppermute | solution.py:73
  68.8 5.1 %collective-permute-start.5 = (bf16[256,768]{1,0:T(8,128)(2,1)S(1)}, bf16[256,768]{1,0:T(8,128)(2,1)S(1)}, u32[]{:S(2)}, u32[]{:S(2)}) collective-permute-start(bf16[256,768]{1,0:T(8,128)(2,1)S(1)} %fusion.20.n_ref), channel_id=1, source_target_pairs={{0,1},{1,0},{2,3},{3,2},{4,5},{5,4},{6,7},{7,6},{8,9},{9,8},{10,11... | collective-permute-start | bytes 1179656 | tf_op jit(solution)/shard_map/ppermute | solution.py:57
  77.3 4.5 collective-permute-done.9
  88.3 14.5 %collective-permute-done.3 = bf16[4,192,384]{2,1,0:T(8,128)(2,1)S(1)} collective-permute-done((bf16[4,192,384]{2,1,0:T(8,128)(2,1)S(1)}, bf16[4,192,384]{2,1,0:T(8,128)(2,1)S(1)}, u32[]{:S(2)}, u32[]{:S(2)}) %collective-permute-start.3) | collective-permute-done | bytes 589856 | tf_op jit(solution)/shard_map/ppermute | solution.py:73
  106.3 4.3 collective-permute-done.24
  110.6 17.4 %collective-permute-done.28 = bf16[4,96,1536]{2,1,0:T(8,128)(2,1)S(1)} collective-permute-done((bf16[4,96,1536]{2,1,0:T(8,128)(2,1)S(1)}, bf16[4,96,1536]{2,1,0:T(8,128)(2,1)S(1)}, u32[]{:S(2)}, u32[]{:S(2)}) %collective-permute-start.28) | collective-permute-done | bytes 1179680 | tf_op jit(solution)/shard_map/ppermute | solution.py:73
  128.3 15.6 %collective-permute-done.11 = bf16[4,96,1536]{2,1,0:T(8,128)(2,1)S(1)} collective-permute-done((bf16[4,96,1536]{2,1,0:T(8,128)(2,1)S(1)}, bf16[4,96,1536]{2,1,0:T(8,128)(2,1)S(1)}, u32[]{:S(2)}, u32[]{:S(2)}) %collective-permute-start.11) | collective-permute-done | bytes 1179680 | tf_op jit(solution)/shard_map/ppermute | solution.py:73
  146.0 3.6 attend_forward.5
  150.0 3.6 attend_forward.4
  164.9 10.6 %collective-permute-done.14 = bf16[64,768]{1,0:T(8,128)(2,1)S(1)} collective-permute-done((bf16[64,768]{1,0:T(8,128)(2,1)S(1)}, bf16[64,768]{1,0:T(8,128)(2,1)S(1)}, u32[]{:S(2)}, u32[]{:S(2)}) %collective-permute-start.14) | collective-permute-done | bytes 98336 | tf_op jit(solution)/shard_map/ppermute | solution.py:57
  179.7 4.2 collective-permute-done.15
  186.2 8.1 %collective-permute-done.21.n_ref = bf16[256,768]{1,0:T(8,128)(2,1)S(1)} collective-permute-done((bf16[256,768]{1,0:T(8,128)(2,1)S(1)}, bf16[256,768]{1,0:T(8,128)(2,1)S(1)}, u32[]{:S(2)}, u32[]{:S(2)}) %collective-permute-start.21) | collective-permute-done | bytes 393248 | tf_op jit(solution)/shard_map/ppermute | solution.py:57
  194.2 3.6 attend_forward.7
  198.3 4.8 mlp_forward.2
  206.0 3.6 attend_forward.6
  211.0 5.4 %collective-permute-done.13 = bf16[256,768]{1,0:T(8,128)(2,1)S(1)} collective-permute-done((bf16[256,768]{1,0:T(8,128)(2,1)S(1)}, bf16[256,768]{1,0:T(8,128)(2,1)S(1)}, u32[]{:S(2)}, u32[]{:S(2)}) %collective-permute-start.13) | collective-permute-done | bytes 393248 | tf_op jit(solution)/shard_map/ppermute | solution.py:57
  218.2 4.4 collective-permute-done.23
  222.6 10.7 %mlp_backward.2 = (bf16[512,768]{1,0:T(8,128)(2,1)S(1)}, bf16[512,768]{1,0:T(8,128)(2,1)S(1)}, bf16[768,1536]{1,0:T(8,128)(2,1)S(1)}, bf16[768,1536]{1,0:T(8,128)(2,1)S(1)}, f32[1,1536]{1,0:T(1,128)S(1)}) custom-call(bf16[512,768]{1,0:T(8,128)(2,1)S(1)} %pad_maximum_fusion.5.n_ref, bf16[512,768]{1,0:T(8,128)(2,1)S(1)} %pad_maximum_fusion.6.g_ref, ...), custom_call_target="tpu_custom_call" | custom-call | flops 7247757312 | bytes 12582912 | tf_op jit(solution)/shard_map/mlp_backward/pallas_call | solution.py:409
  239.0 6.6 %collective-permute-done.31 = bf16[256,768]{1,0:T(8,128)(2,1)S(1)} collective-permute-done((bf16[256,768]{1,0:T(8,128)(2,1)S(1)}, bf16[256,768]{1,0:T(8,128)(2,1)S(1)}, u32[]{:S(2)}, u32[]{:S(2)}) %collective-permute-start.31) | collective-permute-done | bytes 393248 | tf_op jit(solution)/shard_map/ppermute | solution.py:57
  246.0 4.7 collective-permute-done.30
  256.7 4.4 collective-permute-done.32
  267.2 15.0 %attend_backward.2 = (bf16[2,256,768]{2,1,0:T(8,128)(2,1)S(1)}, bf16[3,768,384]{2,1,0:T(8,128)(2,1)S(1)}, bf16[768,384]{1,0:T(8,128)(2,1)S(1)}, f32[2,384]{1,0:T(2,128)S(1)}) custom-call(bf16[2,256,768]{2,1,0:T(8,128)(2,1)S(1)} %copy-done.27, bf16[2,256,384]{2,1,0:T(8,128)(2,1)S(1)} %copy-done.35, bf16[2,256,384]{2,1,0:T(8,128)(2,1)S(1)} %copy-done.34, ...), custom_call_target="tpu_custom_call" | custom-call | flops 2919235584 | bytes 8650752 | tf_op jit(solution)/shard_map/attend_backward/pallas_call | solution.py:295
  283.2 6.9 %collective-permute-done.33 = bf16[256,768]{1,0:T(8,128)(2,1)S(1)} collective-permute-done((bf16[256,768]{1,0:T(8,128)(2,1)S(1)}, bf16[256,768]{1,0:T(8,128)(2,1)S(1)}, u32[]{:S(2)}, u32[]{:S(2)}) %collective-permute-start.33) | collective-permute-done | bytes 393248 | tf_op jit(solution)/shard_map/ppermute | solution.py:57
  301.0 5.7 %mlp_backward.3 = (bf16[128,768]{1,0:T(8,128)(2,1)}, bf16[128,768]{1,0:T(8,128)(2,1)S(1)}, bf16[768,1536]{1,0:T(8,128)(2,1)S(1)}, bf16[768,1536]{1,0:T(8,128)(2,1)S(1)}, f32[1,1536]{1,0:T(1,128)S(1)}) custom-call(bf16[128,768]{1,0:T(8,128)(2,1)S(1)} %copy-done.25, bf16[128,768]{1,0:T(8,128)(2,1)S(1)} %pad_maximum_fusion.23.g_ref, ...), custom_call_target="tpu_custom_call" | custom-call | flops 1811939328 | bytes 10223616 | tf_op jit(solution)/shard_map/mlp_backward/pallas_call | solution.py:409
  323.5 15.0 %attend_backward.3 = (bf16[2,256,768]{2,1,0:T(8,128)(2,1)S(1)}, bf16[3,768,384]{2,1,0:T(8,128)(2,1)S(1)}, bf16[768,384]{1,0:T(8,128)(2,1)S(1)}, f32[2,384]{1,0:T(2,128)S(1)}) custom-call(bf16[2,256,768]{2,1,0:T(8,128)(2,1)S(1)} %copy-done.26, bf16[2,256,384]{2,1,0:T(8,128)(2,1)S(1)} %copy-done.28, bf16[2,256,384]{2,1,0:T(8,128)(2,1)S(1)} %copy-done.29, ...), custom_call_target="tpu_custom_call" | custom-call | flops 2919235584 | bytes 8650752 | tf_op jit(solution)/shard_map/attend_backward/pallas_call | solution.py:295
  343.8 4.5 collective-permute-done.38
  371.2 5.5 %collective-permute-done.50 = bf16[4,192,384]{2,1,0:T(8,128)(2,1)S(1)} collective-permute-done((bf16[4,192,384]{2,1,0:T(8,128)(2,1)S(1)}, bf16[4,192,384]{2,1,0:T(8,128)(2,1)S(1)}, u32[]{:S(2)}, u32[]{:S(2)}) %collective-permute-start.50) | collective-permute-done | bytes 589856 | tf_op jit(solution)/shard_map/ppermute | solution.py:137
  397.0 15.7 %collective-permute-done.45 = bf16[4,192,384]{2,1,0:T(8,128)(2,1)} collective-permute-done((bf16[4,192,384]{2,1,0:T(8,128)(2,1)}, bf16[4,192,384]{2,1,0:T(8,128)(2,1)}, u32[]{:S(2)}, u32[]{:S(2)}) %collective-permute-start.45) | collective-permute-done | bytes 589856 | tf_op jit(solution)/shard_map/ppermute | solution.py:137
  428.0 4.5 collective-permute-done.47
  434.5 20.8 %collective-permute-done.62 = bf16[1,96,1536]{2,1,0:T(8,128)(2,1)S(1)} collective-permute-done((bf16[1,96,1536]{2,1,0:T(8,128)(2,1)S(1)}, bf16[1,96,1536]{2,1,0:T(8,128)(2,1)S(1)}, u32[]{:S(2)}, u32[]{:S(2)}) %collective-permute-start.62) | collective-permute-done | bytes 294944 | tf_op jit(solution)/shard_map/ppermute | solution.py:137
  463.4 20.6 %collective-permute-done.57 = bf16[1,96,1536]{2,1,0:T(8,128)(2,1)S(1)} collective-permute-done((bf16[1,96,1536]{2,1,0:T(8,128)(2,1)S(1)}, bf16[1,96,1536]{2,1,0:T(8,128)(2,1)S(1)}, u32[]{:S(2)}, u32[]{:S(2)}) %collective-permute-start.57) | collective-permute-done | bytes 294944 | tf_op jit(solution)/shard_map/ppermute | solution.py:137
  (484 shorter events, 214.3 us)
Async XLA Ops:
  3.4 64.6 %collective-permute-start.25 = (bf16[1,96,1536]{2,1,0:T(8,128)(2,1)}, bf16[1,96,1536]{2,1,0:T(8,128)(2,1)}, u32[]{:S(2)}, u32[]{:S(2)}) collective-permute-start(bf16[1,96,1536]{2,1,0:T(8,128)(2,1)} %maximum_bitcast_fusion.3), channel_id=1, source_target_pairs={{0,8},{2,10},{4,12},{6,14},{8,16},{10,18},{12,20},{14,22},{16,24},... | collective-permute-start | bytes 884744 | tf_op jit(solution)/shard_map/ppermute | solution.py:73
  3.4 65.4 %collective-permute-start.26 = (bf16[1,96,1536]{2,1,0:T(8,128)(2,1)}, bf16[1,96,1536]{2,1,0:T(8,128)(2,1)}, u32[]{:S(2)}, u32[]{:S(2)}) collective-permute-start(bf16[1,96,1536]{2,1,0:T(8,128)(2,1)} %maximum_bitcast_fusion.3), channel_id=1, source_target_pairs={{0,16},{2,18},{4,20},{6,22},{8,24},{10,26},{12,28},{14,30},{16,0},... | collective-permute-start | bytes 884744 | tf_op jit(solution)/shard_map/ppermute | solution.py:73
  7.8 23.8 %collective-permute-start.16 = (bf16[1,192,384]{2,1,0:T(8,128)(2,1)}, bf16[1,192,384]{2,1,0:T(8,128)(2,1)}, u32[]{:S(2)}, u32[]{:S(2)}) collective-permute-start(bf16[1,192,384]{2,1,0:T(8,128)(2,1)} %maximum_bitcast_fusion.5), channel_id=1, source_target_pairs={{0,8},{2,10},{4,12},{6,14},{8,16},{10,18},{12,20},{14,22},{16,24},... | collective-permute-start | bytes 442376 | tf_op jit(solution)/shard_map/ppermute | solution.py:73
  10.2 34.8 %collective-permute-start.17 = (bf16[1,192,384]{2,1,0:T(8,128)(2,1)}, bf16[1,192,384]{2,1,0:T(8,128)(2,1)}, u32[]{:S(2)}, u32[]{:S(2)}) collective-permute-start(bf16[1,192,384]{2,1,0:T(8,128)(2,1)} %maximum_bitcast_fusion.5), channel_id=1, source_target_pairs={{0,16},{2,18},{4,20},{6,22},{8,24},{10,26},{12,28},{14,30},{16,0},... | collective-permute-start | bytes 442376 | tf_op jit(solution)/shard_map/ppermute | solution.py:73
  10.2 19.3 %collective-permute-start.36 = (s32[1,64]{1,0:T(1,128)}, s32[1,64]{1,0:T(1,128)}, u32[]{:S(2)}, u32[]{:S(2)}) collective-permute-start(s32[1,64]{1,0:T(1,128)} %param.15), channel_id=1, source_target_pairs={{0,1},{1,0},{2,3},{3,2},{4,5},{5,4},{6,7},{7,6},{8,9},{9,8},{10,11... | collective-permute-start | bytes 776 | tf_op jit(solution)/shard_map/ppermute | solution.py:57
  29.5 15.6 %collective-permute-start.18 = (bf16[1,192,384]{2,1,0:T(8,128)(2,1)}, bf16[1,192,384]{2,1,0:T(8,128)(2,1)S(1)}, u32[]{:S(2)}, u32[]{:S(2)}) collective-permute-start(bf16[1,192,384]{2,1,0:T(8,128)(2,1)} %maximum_bitcast_fusion.5), channel_id=1, source_target_pairs={{0,24},{2,26},{4,28},{6,30},{8,0},{10,2},{12,4},{14,6},{16,8},{18,... | collective-permute-start | bytes 442376 | tf_op jit(solution)/shard_map/ppermute | solution.py:73
  31.5 42.3 %collective-permute-start.27 = (bf16[1,96,1536]{2,1,0:T(8,128)(2,1)}, bf16[1,96,1536]{2,1,0:T(8,128)(2,1)S(1)}, u32[]{:S(2)}, u32[]{:S(2)}) collective-permute-start(bf16[1,96,1536]{2,1,0:T(8,128)(2,1)} %maximum_bitcast_fusion.3), channel_id=1, source_target_pairs={{0,24},{2,26},{4,28},{6,30},{8,0},{10,2},{12,4},{14,6},{16,8},{18,... | collective-permute-start | bytes 884744 | tf_op jit(solution)/shard_map/ppermute | solution.py:73
  56.3 20.4 %collective-permute-start.8 = (bf16[1,96,1536]{2,1,0:T(8,128)(2,1)S(1)}, bf16[1,96,1536]{2,1,0:T(8,128)(2,1)S(1)}, u32[]{:S(2)}, u32[]{:S(2)}) collective-permute-start(bf16[1,96,1536]{2,1,0:T(8,128)(2,1)S(1)} %copy-done.59), channel_id=1, source_target_pairs={{0,8},{2,10},{4,12},{6,14},{8,16},{10,18},{12,20},{14,22},{16,24},... | collective-permute-start | bytes 884744 | tf_op jit(solution)/shard_map/ppermute | solution.py:73
  60.6 21.2 %collective-permute-start.9 = (bf16[1,96,1536]{2,1,0:T(8,128)(2,1)S(1)}, bf16[1,96,1536]{2,1,0:T(8,128)(2,1)S(1)}, u32[]{:S(2)}, u32[]{:S(2)}) collective-permute-start(bf16[1,96,1536]{2,1,0:T(8,128)(2,1)S(1)} %copy-done.59), channel_id=1, source_target_pairs={{0,16},{2,18},{4,20},{6,22},{8,24},{10,26},{12,28},{14,30},{16,0},... | collective-permute-start | bytes 884744 | tf_op jit(solution)/shard_map/ppermute | solution.py:73
  68.8 35.9 %collective-permute-start.5 = (bf16[256,768]{1,0:T(8,128)(2,1)S(1)}, bf16[256,768]{1,0:T(8,128)(2,1)S(1)}, u32[]{:S(2)}, u32[]{:S(2)}) collective-permute-start(bf16[256,768]{1,0:T(8,128)(2,1)S(1)} %fusion.20.n_ref), channel_id=1, source_target_pairs={{0,1},{1,0},{2,3},{3,2},{4,5},{5,4},{6,7},{7,6},{8,9},{9,8},{10,11... | collective-permute-start | bytes 1179656 | tf_op jit(solution)/shard_map/ppermute | solution.py:57
  73.9 29.8 %collective-permute-start.19 = (bf16[4,192,384]{2,1,0:T(8,128)(2,1)S(1)}, bf16[4,192,384]{2,1,0:T(8,128)(2,1)S(1)}, u32[]{:S(2)}, u32[]{:S(2)}) collective-permute-start(bf16[4,192,384]{2,1,0:T(8,128)(2,1)S(1)} %pad_maximum_fusion.12), channel_id=1, source_target_pairs={{0,4},{2,6},{4,0},{6,2},{8,12},{10,14},{12,8},{14,10},{16,20},{18,... | collective-permute-start | bytes 1769480 | tf_op jit(solution)/shard_map/ppermute | solution.py:73
  76.7 26.1 %collective-permute-start.3 = (bf16[4,192,384]{2,1,0:T(8,128)(2,1)S(1)}, bf16[4,192,384]{2,1,0:T(8,128)(2,1)S(1)}, u32[]{:S(2)}, u32[]{:S(2)}) collective-permute-start(bf16[4,192,384]{2,1,0:T(8,128)(2,1)S(1)} %pad_maximum_fusion.11), channel_id=1, source_target_pairs={{0,4},{2,6},{4,0},{6,2},{8,12},{10,14},{12,8},{14,10},{16,20},{18,... | collective-permute-start | bytes 1769480 | tf_op jit(solution)/shard_map/ppermute | solution.py:73
  81.8 46.3 %collective-permute-start.28 = (bf16[4,96,1536]{2,1,0:T(8,128)(2,1)S(1)}, bf16[4,96,1536]{2,1,0:T(8,128)(2,1)S(1)}, u32[]{:S(2)}, u32[]{:S(2)}) collective-permute-start(bf16[4,96,1536]{2,1,0:T(8,128)(2,1)S(1)} %pad_maximum_fusion.3), channel_id=1, source_target_pairs={{0,4},{2,6},{4,0},{6,2},{8,12},{10,14},{12,8},{14,10},{16,20},{18,... | collective-permute-start | bytes 3538952 | tf_op jit(solution)/shard_map/ppermute | solution.py:73
  83.4 60.5 %collective-permute-start.11 = (bf16[4,96,1536]{2,1,0:T(8,128)(2,1)S(1)}, bf16[4,96,1536]{2,1,0:T(8,128)(2,1)S(1)}, u32[]{:S(2)}, u32[]{:S(2)}) collective-permute-start(bf16[4,96,1536]{2,1,0:T(8,128)(2,1)S(1)} %pad_maximum_fusion.2), channel_id=1, source_target_pairs={{0,4},{2,6},{4,0},{6,2},{8,12},{10,14},{12,8},{14,10},{16,20},{18,... | collective-permute-start | bytes 3538952 | tf_op jit(solution)/shard_map/ppermute | solution.py:73
  103.7 40.5 %collective-permute-start.4 = (bf16[8,192,384]{2,1,0:T(8,128)(2,1)}, bf16[8,192,384]{2,1,0:T(8,128)(2,1)S(1)}, u32[]{:S(2)}, u32[]{:S(2)}) collective-permute-start(bf16[8,192,384]{2,1,0:T(8,128)(2,1)} %get-tuple-element.167), channel_id=1, source_target_pairs={{0,2},{2,0},{4,6},{6,4},{8,10},{10,8},{12,14},{14,12},{16,18},{18,... | collective-permute-start | bytes 3538952 | tf_op jit(solution)/shard_map/ppermute | solution.py:73
  104.7 49.0 %collective-permute-start.20 = (bf16[8,192,384]{2,1,0:T(8,128)(2,1)}, bf16[8,192,384]{2,1,0:T(8,128)(2,1)S(1)}, u32[]{:S(2)}, u32[]{:S(2)}) collective-permute-start(bf16[8,192,384]{2,1,0:T(8,128)(2,1)} %get-tuple-element.165), channel_id=1, source_target_pairs={{0,2},{2,0},{4,6},{6,4},{8,10},{10,8},{12,14},{14,12},{16,18},{18,... | collective-permute-start | bytes 3538952 | tf_op jit(solution)/shard_map/ppermute | solution.py:73
  128.3 57.7 %collective-permute-start.29 = (bf16[8,96,1536]{2,1,0:T(8,128)(2,1)S(1)}, bf16[8,96,1536]{2,1,0:T(8,128)(2,1)S(1)}, u32[]{:S(2)}, u32[]{:S(2)}) collective-permute-start(bf16[8,96,1536]{2,1,0:T(8,128)(2,1)S(1)} %get-tuple-element.156), channel_id=1, source_target_pairs={{0,2},{2,0},{4,6},{6,4},{8,10},{10,8},{12,14},{14,12},{16,18},{18,... | collective-permute-start | bytes 7077896 | tf_op jit(solution)/shard_map/ppermute | solution.py:73
  144.2 31.4 %collective-permute-start.12 = (bf16[8,96,1536]{2,1,0:T(8,128)(2,1)S(1)}, bf16[8,96,1536]{2,1,0:T(8,128)(2,1)S(1)}, u32[]{:S(2)}, u32[]{:S(2)}) collective-permute-start(bf16[8,96,1536]{2,1,0:T(8,128)(2,1)S(1)} %get-tuple-element.158), channel_id=1, source_target_pairs={{0,2},{2,0},{4,6},{6,4},{8,10},{10,8},{12,14},{14,12},{16,18},{18,... | collective-permute-start | bytes 7077896 | tf_op jit(solution)/shard_map/ppermute | solution.py:73
  162.7 23.3 %collective-permute-start.7 = (bf16[256,768]{1,0:T(8,128)(2,1)S(1)}, bf16[256,768]{1,0:T(8,128)(2,1)S(1)}, u32[]{:S(2)}, u32[]{:S(2)}) collective-permute-start(bf16[256,768]{1,0:T(8,128)(2,1)S(1)} %add_convert_fusion.4), channel_id=1, source_target_pairs={{0,1},{1,0},{2,3},{3,2},{4,5},{5,4},{6,7},{7,6},{8,9},{9,8},{10,11... | collective-permute-start | bytes 1179656 | tf_op jit(solution)/shard_map/ppermute | solution.py:57
  254.8 111.3 %collective-permute-start.59 = (bf16[8,96,1536]{2,1,0:T(8,128)(2,1)}, bf16[8,96,1536]{2,1,0:T(8,128)(2,1)}, u32[]{:S(2)}, u32[]{:S(2)}) collective-permute-start(bf16[8,96,1536]{2,1,0:T(8,128)(2,1)} %fusion.1), channel_id=1, source_target_pairs={{0,2},{2,0},{4,6},{6,4},{8,10},{10,8},{12,14},{14,12},{16,18},{18,... | collective-permute-start | bytes 7077896 | tf_op jit(solution)/shard_map/ppermute | solution.py:137
  295.4 61.6 %collective-permute-start.49 = (bf16[8,192,384]{2,1,0:T(8,128)(2,1)}, bf16[8,192,384]{2,1,0:T(8,128)(2,1)}, u32[]{:S(2)}, u32[]{:S(2)}) collective-permute-start(bf16[8,192,384]{2,1,0:T(8,128)(2,1)} %dynamic-slice_bitcast_fusion), channel_id=1, source_target_pairs={{0,2},{2,0},{4,6},{6,4},{8,10},{10,8},{12,14},{14,12},{16,18},{18,... | collective-permute-start | bytes 3538952 | tf_op jit(solution)/shard_map/ppermute | solution.py:137
  310.2 111.1 %collective-permute-start.54 = (bf16[8,96,1536]{2,1,0:T(8,128)(2,1)}, bf16[8,96,1536]{2,1,0:T(8,128)(2,1)}, u32[]{:S(2)}, u32[]{:S(2)}) collective-permute-start(bf16[8,96,1536]{2,1,0:T(8,128)(2,1)} %fusion.5), channel_id=1, source_target_pairs={{0,2},{2,0},{4,6},{6,4},{8,10},{10,8},{12,14},{14,12},{16,18},{18,... | collective-permute-start | bytes 7077896 | tf_op jit(solution)/shard_map/ppermute | solution.py:137
  343.7 37.0 %collective-permute-start.44 = (bf16[8,192,384]{2,1,0:T(8,128)(2,1)}, bf16[8,192,384]{2,1,0:T(8,128)(2,1)}, u32[]{:S(2)}, u32[]{:S(2)}) collective-permute-start(bf16[8,192,384]{2,1,0:T(8,128)(2,1)} %dynamic-slice_bitcast_fusion.1), channel_id=1, source_target_pairs={{0,2},{2,0},{4,6},{6,4},{8,10},{10,8},{12,14},{14,12},{16,18},{18,... | collective-permute-start | bytes 3538952 | tf_op jit(solution)/shard_map/ppermute | solution.py:137
  360.3 16.3 %collective-permute-start.50 = (bf16[4,192,384]{2,1,0:T(8,128)(2,1)S(1)}, bf16[4,192,384]{2,1,0:T(8,128)(2,1)S(1)}, u32[]{:S(2)}, u32[]{:S(2)}) collective-permute-start(bf16[4,192,384]{2,1,0:T(8,128)(2,1)S(1)} %fusion.37), channel_id=1, source_target_pairs={{0,4},{2,6},{4,0},{6,2},{8,12},{10,14},{12,8},{14,10},{16,20},{18,... | collective-permute-start | bytes 1769480 | tf_op jit(solution)/shard_map/ppermute | solution.py:137
  363.9 23.4 %collective-permute-start.43 = (f32[13824]{0:T(1024)S(1)}, f32[13824]{0:T(1024)S(1)}, u32[]{:S(2)}, u32[]{:S(2)}) collective-permute-start(f32[13824]{0:T(1024)S(1)} %add.574), channel_id=1, source_target_pairs={{0,16},{2,18},{4,20},{6,22},{8,24},{10,26},{12,28},{14,30},{16,0},... | collective-permute-start | bytes 165896 | tf_op jit(solution)/shard_map/ppermute | solution.py:150
  369.7 49.9 %collective-permute-start.60 = (bf16[4,96,1536]{2,1,0:T(8,128)(2,1)}, bf16[4,96,1536]{2,1,0:T(8,128)(2,1)}, u32[]{:S(2)}, u32[]{:S(2)}) collective-permute-start(bf16[4,96,1536]{2,1,0:T(8,128)(2,1)} %fusion.12), channel_id=1, source_target_pairs={{0,4},{2,6},{4,0},{6,2},{8,12},{10,14},{12,8},{14,10},{16,20},{18,... | collective-permute-start | bytes 3538952 | tf_op jit(solution)/shard_map/ppermute | solution.py:137
  383.1 29.6 %collective-permute-start.45 = (bf16[4,192,384]{2,1,0:T(8,128)(2,1)}, bf16[4,192,384]{2,1,0:T(8,128)(2,1)}, u32[]{:S(2)}, u32[]{:S(2)}) collective-permute-start(bf16[4,192,384]{2,1,0:T(8,128)(2,1)} %fusion.36), channel_id=1, source_target_pairs={{0,4},{2,6},{4,0},{6,2},{8,12},{10,14},{12,8},{14,10},{16,20},{18,... | collective-permute-start | bytes 1769480 | tf_op jit(solution)/shard_map/ppermute | solution.py:137
  423.7 31.7 %collective-permute-start.55 = (bf16[4,96,1536]{2,1,0:T(8,128)(2,1)S(1)}, bf16[4,96,1536]{2,1,0:T(8,128)(2,1)S(1)}, u32[]{:S(2)}, u32[]{:S(2)}) collective-permute-start(bf16[4,96,1536]{2,1,0:T(8,128)(2,1)S(1)} %fusion.11), channel_id=1, source_target_pairs={{0,4},{2,6},{4,0},{6,2},{8,12},{10,14},{12,8},{14,10},{16,20},{18,... | collective-permute-start | bytes 3538952 | tf_op jit(solution)/shard_map/ppermute | solution.py:137
  427.0 28.3 %collective-permute-start.62 = (bf16[1,96,1536]{2,1,0:T(8,128)(2,1)S(1)}, bf16[1,96,1536]{2,1,0:T(8,128)(2,1)S(1)}, u32[]{:S(2)}, u32[]{:S(2)}) collective-permute-start(bf16[1,96,1536]{2,1,0:T(8,128)(2,1)S(1)} %get-tuple-element.143), channel_id=1, source_target_pairs={{0,16},{2,18},{4,20},{6,22},{8,24},{10,26},{12,28},{14,30},{16,0},... | collective-permute-start | bytes 884744 | tf_op jit(solution)/shard_map/ppermute | solution.py:137
  432.5 22.8 %collective-permute-start.63 = (bf16[1,96,1536]{2,1,0:T(8,128)(2,1)S(1)}, bf16[1,96,1536]{2,1,0:T(8,128)(2,1)S(1)}, u32[]{:S(2)}, u32[]{:S(2)}) collective-permute-start(bf16[1,96,1536]{2,1,0:T(8,128)(2,1)S(1)} %get-tuple-element.142), channel_id=1, source_target_pairs={{0,24},{2,26},{4,28},{6,30},{8,0},{10,2},{12,4},{14,6},{16,8},{18,... | collective-permute-start | bytes 884744 | tf_op jit(solution)/shard_map/ppermute | solution.py:137
  455.9 28.1 %collective-permute-start.57 = (bf16[1,96,1536]{2,1,0:T(8,128)(2,1)S(1)}, bf16[1,96,1536]{2,1,0:T(8,128)(2,1)S(1)}, u32[]{:S(2)}, u32[]{:S(2)}) collective-permute-start(bf16[1,96,1536]{2,1,0:T(8,128)(2,1)S(1)} %get-tuple-element.140), channel_id=1, source_target_pairs={{0,16},{2,18},{4,20},{6,22},{8,24},{10,26},{12,28},{14,30},{16,0},... | collective-permute-start | bytes 884744 | tf_op jit(solution)/shard_map/ppermute | solution.py:137
  458.0 26.1 %collective-permute-start.58 = (bf16[1,96,1536]{2,1,0:T(8,128)(2,1)S(1)}, bf16[1,96,1536]{2,1,0:T(8,128)(2,1)S(1)}, u32[]{:S(2)}, u32[]{:S(2)}) collective-permute-start(bf16[1,96,1536]{2,1,0:T(8,128)(2,1)S(1)} %get-tuple-element.139), channel_id=1, source_target_pairs={{0,24},{2,26},{4,28},{6,30},{8,0},{10,2},{12,4},{14,6},{16,8},{18,... | collective-permute-start | bytes 884744 | tf_op jit(solution)/shard_map/ppermute | solution.py:137
  (119 other events, 1385.7 us)

commit v2 on v0

v2 whole, which is shorter than its diff:
```python
from functools import partial

import jax
import jax.numpy as jnp
from jax import lax
from jax.experimental import pallas as pl
from jax.experimental.pallas import tpu as pltpu
from jax.sharding import PartitionSpec as P

HEAD = 64
LANES = 128
BLOCK = 48
EPSILON = 1e-05
BF = jnp.bfloat16
F32 = jnp.float32
GELU_C = 0.7978845608028654
GELU_A = 0.044715
MIB = 1 << 20


def dot(a, b):
    return lax.dot_general(a, b, (((1,), (0,)), ((), ())), preferred_element_type=F32)


def dot_nt(a, b):
    return lax.dot_general(a, b, (((1,), (1,)), ((), ())), preferred_element_type=F32)


def dot_tn(a, b):
    return lax.dot_general(a, b, (((0,), (0,)), ((), ())), preferred_element_type=F32)


def vmem(mib):
    return pltpu.CompilerParams(vmem_limit_bytes=mib * MIB)


def cost(flops, moved, exps=0):
    return pl.CostEstimate(flops=flops, transcendentals=exps, bytes_accessed=moved)


VMEM = pl.BlockSpec(memory_space=pltpu.VMEM)


def shape(dims, kind):
    return jax.ShapeDtypeStruct(tuple(dims), kind)


def across(value, count, stride):
    return lax.ppermute(value, "fsdp", [(place, place ^ stride) for place in range(count)])


def swap(value):
    return lax.ppermute(value, "tensor", [(0, 1), (1, 0)])


def after(value, *others):
    leaves, tree = jax.tree.flatten(value)
    held = lax.optimization_barrier(tuple(leaves) + tuple(jax.tree.leaves(others)))
    return jax.tree.unflatten(tree, held[: len(leaves)])


def join_kernel(own_ref, got_ref, out_ref):
    half = out_ref.shape[0] // 2
    for index in range(half):
        out_ref[index] = own_ref[index] if own_ref.ndim == 3 else own_ref[...]
        out_ref[half + index] = got_ref[index] if got_ref.ndim == 3 else got_ref[...]


def join(own, got):
    dims = own.shape[-2:]
    blocks = 2 if own.ndim == 2 else 2 * own.shape[0]
    return pl.pallas_call(
        join_kernel,
        name="join",
        out_shape=shape((blocks,) + dims, BF),
        in_specs=[VMEM] * 2,
        compiler_params=vmem(4),
        cost_estimate=cost(0, 4 * blocks * dims[0] * dims[1]),
    )(own, got)


def load_blocks(bufs, target, columns=None):
    if len(bufs) == 1:
        target[...] = bufs[0][...] if columns is None else bufs[0][:, :, columns]
        return
    me = lax.axis_index("fsdp")
    for number, buf in enumerate(bufs):
        for block in range(buf.shape[0]):
            away = (number // 2) + 2 * (number % 2) + 4 * (block // 2) + 8 * (block % 2)
            at = jnp.bitwise_xor(me, away)
            target[at] = buf[block] if columns is None else buf[block, :, columns]


def store_blocks(value, outs, rows, columns=slice(None)):
    if len(outs) == 1:
        outs[0][:, rows, columns] = value
        return
    pairs = value.reshape((value.shape[0] // 2, 2) + value.shape[1:])
    first = lax.rem(lax.axis_index("fsdp"), 2) == 0
    outs[0][:, rows, columns] = jnp.where(first, pairs[:, 0], pairs[:, 1])
    outs[1][:, rows, columns] = jnp.where(first, pairs[:, 1], pairs[:, 0])


def row_of(ref, layer, which):
    return ref[layer].astype(F32)[which : which + 1, :]


def statistics(rows):
    mean = jnp.mean(rows, axis=-1, keepdims=True)
    center = rows - mean
    scale = lax.rsqrt(jnp.mean(center * center, axis=-1, keepdims=True) + EPSILON)
    return (center * scale, scale)


def norm_backward(rows, grad, gain):
    unit, scale = statistics(rows)
    e = grad * gain
    back = scale * (
        e
        - jnp.mean(e, axis=-1, keepdims=True)
        - unit * jnp.mean(e * unit, axis=-1, keepdims=True)
    )
    return (
        back,
        jnp.sum(grad * unit, axis=0, keepdims=True),
        jnp.sum(grad, axis=0, keepdims=True),
    )


def column(row):
    wide = jnp.broadcast_to(row.astype(F32), (8, row.shape[1]))
    return wide.T[:, 0:1]


def place_rows(slots_ref, less, seq):
    slots = slots_ref.shape[1]
    wanted = column(slots_ref[...]) - float(less)
    places = lax.broadcasted_iota(jnp.int32, (slots, seq), 1).astype(F32)
    return wanted == places


def place_columns(slots_ref, less, seq):
    slots = slots_ref.shape[1]
    wanted = slots_ref[...] - less
    places = lax.broadcasted_iota(jnp.int32, (seq, slots), 0)
    return wanted == places


def ones(hit):
    return jnp.where(hit, 1.0, 0.0).astype(BF)


def exact_pick(hit, value):
    high = value.astype(BF)
    rest = value - high.astype(F32)
    middle = rest.astype(BF)
    low = (rest - middle.astype(F32)).astype(BF)
    return dot(hit, high) + dot(hit, middle) + dot(hit, low)


def start_kernel(jt_ref, mt_ref, x_ref, gain_ref, shift_ref, a_ref, n_ref, x_buf, sems):
    rows = mt_ref.shape[1]
    copies = [
        pltpu.make_async_copy(
            jt_ref.at[0, which], a_ref.at[which * rows : (which + 1) * rows], sems.at[which]
        )
        for which in range(3)
    ]
    copies.append(pltpu.make_async_copy(mt_ref.at[0], a_ref.at[3 * rows : 4 * rows], sems.at[3]))
    copies.append(pltpu.make_async_copy(x_ref, x_buf, sems.at[4]))
    for copy in copies[::-1]:
        copy.start()
    copies[4].wait()
    unit, _ = statistics(x_buf[...].astype(F32))
    n_ref[...] = (unit * row_of(gain_ref, 0, 0) + row_of(shift_ref, 0, 0)).astype(BF)
    for copy in copies[:4]:
        copy.wait()


def start(jt, mt, x, gains, shifts):
    rows, width = mt.shape[1:]
    hbm = pl.BlockSpec(memory_space=pltpu.HBM)
    return pl.pallas_call(
        start_kernel,
        name="start",
        out_shape=[shape((4 * rows, width), BF), shape(x.shape, BF)],
        in_specs=[hbm] * 3 + [VMEM] * 2,
        out_specs=[VMEM] * 2,
        scratch_shapes=[pltpu.VMEM(x.shape, BF), pltpu.SemaphoreType.DMA((5,))],
        compiler_params=vmem(8),
        cost_estimate=cost(0, 8 * rows * width + 4 * x.size),
    )(jt, mt, x, gains, shifts)


def rest_kernel(jt_ref, mt_ref, ex_ref, sh_ref, *refs):
    e0_ref, s0_ref, a1_ref, e1_ref, s1_ref, sems = refs
    rows = mt_ref.shape[1]
    pairs = [(ex_ref.at[0], e0_ref), (sh_ref.at[0], s0_ref)]
    pairs += [(jt_ref.at[1, which], a1_ref.at[which * rows : (which + 1) * rows]) for which in range(3)]
    pairs += [(mt_ref.at[1], a1_ref.at[3 * rows : 4 * rows])]
    pairs += [(ex_ref.at[1], e1_ref), (sh_ref.at[1], s1_ref)]
    copies = [
        pltpu.make_async_copy(source, target, sems.at[index])
        for index, (source, target) in enumerate(pairs)
    ]
    for copy in copies:
        copy.start()
    for copy in copies:
        copy.wait()


def rest(jt, mt, ex, sh):
    rows, width = mt.shape[1:]
    plain = shape((rows, ex.shape[2]), BF)
    return pl.pallas_call(
        rest_kernel,
        name="rest",
        out_shape=[plain, plain, shape((4 * rows, width), BF), plain, plain],
        in_specs=[pl.BlockSpec(memory_space=pltpu.HBM)] * 4,
        out_specs=[VMEM] * 5,
        scratch_shapes=[pltpu.SemaphoreType.DMA((8,))],
        compiler_params=vmem(4),
        cost_estimate=cost(0, 8 * rows * width + 16 * rows * ex.shape[2]),
    )(jt, mt, ex, sh)


def segment_row(seg_ref, peer):
    mine = lax.axis_index("tensor")
    which = (1 - mine) if peer else mine
    both = seg_ref[...].astype(F32)
    row = jnp.where(which == 0, both[0:1, :], both[1:2, :])
    return row


def lane_masks(rows):
    lane = lax.broadcasted_iota(jnp.int32, (rows, LANES), 1)
    return (lane < HEAD, lane >= HEAD)


def attend_forward_kernel(count, layer, peer, arrays, n_ref, seg_ref, bias_ref, *refs):
    bufs = refs[:arrays]
    part_ref, q_ref, k_ref, v_ref, mixed_ref, w_ref, neg_ref = refs[arrays:]
    load_blocks(bufs, w_ref)
    seq, d = n_ref.shape
    width = q_ref.shape[1]
    half = seq // 2
    row = segment_row(seg_ref, peer)
    rows = lax.broadcasted_iota(jnp.int32, (seq, seq), 0)
    cols = lax.broadcasted_iota(jnp.int32, (seq, seq), 1)
    allowed = (column(row) == row) & (cols <= rows)
    neg_ref[...] = jnp.where(allowed, 0.0, -1e30)
    n = n_ref[...]

    def weight(which):
        return w_ref[:, which * BLOCK : (which + 1) * BLOCK, :].reshape(d, width)

    q_ref[...] = (dot(n, weight(0)) + row_of(bias_ref, layer, 0)).astype(BF)
    k_ref[...] = dot(n, weight(1)).astype(BF)
    v_ref[...] = (dot(n, weight(2)) + row_of(bias_ref, layer, 1)).astype(BF)
    masks = lane_masks(half)
    for pair in range(width // LANES):
        lanes = slice(pair * LANES, (pair + 1) * LANES)
        for part in range(2):
            top = slice(part * half, (part + 1) * half)
            keys = slice(0, (part + 1) * half)
            qp = q_ref[top, lanes] * BF(HEAD ** (-0.5))
            kp = k_ref[keys, lanes]
            vp = v_ref[keys, lanes]
            found = []
            for mask in masks:
                s = dot_nt(jnp.where(mask, qp, BF(0)), kp) + neg_ref[top, keys]
                e = jnp.exp(s - jnp.max(s, axis=-1, keepdims=True))
                scale = 1.0 / jnp.sum(e, axis=-1, keepdims=True)
                found.append(dot((e * scale).astype(BF), vp))
            mixed_ref[top, lanes] = jnp.where(masks[0], found[0], found[1]).astype(BF)
    part_ref[...] = dot_nt(mixed_ref[...], weight(3)).astype(BF)


def attend_forward(count, layer, peer, n, segments, bias, bufs):
    seq, d = n.shape
    width = bufs[0].shape[-1]
    rows = shape((seq, width), BF)
    return pl.pallas_call(
        partial(attend_forward_kernel, count, layer, peer, len(bufs)),
        name="attend_forward",
        out_shape=[shape((seq, d), BF), rows, rows, rows, rows],
        in_specs=[VMEM] * (3 + len(bufs)),
        scratch_shapes=[
            pltpu.VMEM((d // BLOCK, 4 * BLOCK, width), BF),
            pltpu.VMEM((seq, seq), F32),
        ],
        compiler_params=vmem(16),
        cost_estimate=cost(
            8 * seq * d * width + 4 * seq * seq * width,
            8 * d * width + 4 * seq * d + 8 * seq * width,
            seq * seq * width // HEAD,
        ),
    )(n, segments, bias, *bufs)


def attend_backward_kernel(
    count, layer, peer, picked, arrays,
    q_ref, k_ref, v_ref, gm_ref, seg_ref, slots_ref, *refs,
):
    bufs = refs[:arrays]
    refs = refs[arrays:]
    if picked:
        gn_ref, dj_ref, gb_ref, wide_ref, w_ref, neg_ref, gx_ref, qx_ref = refs
    else:
        gn_ref, dj_ref, gb_ref, w_ref, neg_ref, gx_ref = refs
    load_blocks(bufs, w_ref)
    seq, width = q_ref.shape
    d = gm_ref.shape[1]
    half = seq // 2
    row = segment_row(seg_ref, peer)
    if picked:
        slots = gm_ref.shape[0]
        hit = place_rows(slots_ref, 1, seq)
        at = column(slots_ref[...]) - 1.0
        own = jnp.sum(jnp.where(hit, row, 0.0), axis=-1, keepdims=True)
        cols = lax.broadcasted_iota(jnp.int32, (slots, seq), 1).astype(F32)
        neg_ref[...] = jnp.where((own == row) & (cols <= at), 0.0, -1e30)
        qx_ref[...] = dot(ones(hit), q_ref[...]).astype(BF)
        parts = [(slice(0, slots), slice(0, seq))]
        queries = qx_ref
    else:
        rows = lax.broadcasted_iota(jnp.int32, (seq, seq), 0)
        cols = lax.broadcasted_iota(jnp.int32, (seq, seq), 1)
        allowed = (column(row) == row) & (cols <= rows)
        neg_ref[...] = jnp.where(allowed, 0.0, -1e30)
        parts = [
            (slice(part * half, (part + 1) * half), slice(0, (part + 1) * half))
            for part in range(2)
        ]
        queries = q_ref

    def weight(which):
        return w_ref[:, which * BLOCK : (which + 1) * BLOCK, :].reshape(d, width)

    gx_ref[...] = dot(gm_ref[...], weight(3)).astype(BF)
    if picked:
        back = ones(place_columns(slots_ref, 1, seq))
        wide_ref[...] = dot(back, gm_ref[...]).astype(BF)
    masks = lane_masks(parts[0][0].stop)
    for pair in range(width // LANES):
        lanes = slice(pair * LANES, (pair + 1) * LANES)
        dk = [None, None]
        dv = [None, None]
        dq_all = []
        for top, keys in parts:
            qp = queries[top, lanes]
            kp = k_ref[keys, lanes]
            vp = v_ref[keys, lanes]
            gp = gx_ref[top, lanes]
            dq, dk_now, dv_now = [], [], []
            for mask in masks:
                qm = jnp.where(mask, qp, BF(0)) * BF(HEAD ** (-0.5))
                s = dot_nt(qm, kp) + neg_ref[top, keys]
                e = jnp.exp(s - jnp.max(s, axis=-1, keepdims=True))
                p = e * (1.0 / jnp.sum(e, axis=-1, keepdims=True))
                gprobs = dot_nt(jnp.where(mask, gp, BF(0)), vp)
                inner = jnp.sum(gprobs * p, axis=-1, keepdims=True)
                ds = (p * (gprobs - inner) * HEAD ** (-0.5)).astype(BF)
                dq.append(dot(ds, kp))
                dk_now.append(dot_tn(ds, qp))
                dv_now.append(dot_tn(p.astype(BF), gp))
            dq_all.append(jnp.where(masks[0], dq[0], dq[1]))
            key_mask = lane_masks(half)[0]
            for block in range(keys.stop // half):
                at = slice(block * half, (block + 1) * half)
                k_new = jnp.where(key_mask, dk_now[0][at], dk_now[1][at])
                v_new = jnp.where(key_mask, dv_now[0][at], dv_now[1][at])
                dk[block] = k_new if dk[block] is None else dk[block] + k_new
                dv[block] = v_new if dv[block] is None else dv[block] + v_new
        gb_ref[0:1, lanes] = sum(jnp.sum(one, axis=0, keepdims=True) for one in dq_all)
        gb_ref[1:2, lanes] = sum(jnp.sum(one, axis=0, keepdims=True) for one in dv)
        if picked:
            dj_ref[0, :, lanes] = dot(back, dq_all[0].astype(BF)).astype(BF)
        else:
            for (top, _), one in zip(parts, dq_all):
                dj_ref[0, top, lanes] = one.astype(BF)
        for block in range(2):
            at = slice(block * half, (block + 1) * half)
            dj_ref[1, at, lanes] = dk[block].astype(BF)
            dj_ref[2, at, lanes] = dv[block].astype(BF)
    gn = dot_nt(dj_ref[0], weight(0))
    gn = gn + dot_nt(dj_ref[1], weight(1))
    gn = gn + dot_nt(dj_ref[2], weight(2))
    gn_ref[...] = gn.astype(BF)


def attend_backward(count, layer, peer, kept, gm, segments, slots, bufs, picked):
    q, k, v = kept
    seq, width = q.shape
    rows, d = gm.shape
    outs = [shape((seq, d), BF), shape((3, seq, width), BF), shape((2, width), F32)]
    scratch = [
        pltpu.VMEM((d // BLOCK, 4 * BLOCK, width), BF),
        pltpu.VMEM((rows, seq), F32),
        pltpu.VMEM((rows, width), BF),
    ]
    if picked:
        outs.append(shape((seq, d), BF))
        scratch.append(pltpu.VMEM((rows, width), BF))
    return pl.pallas_call(
        partial(attend_backward_kernel, count, layer, peer, picked, len(bufs)),
        name="attend_backward",
        out_shape=outs,
        in_specs=[VMEM] * (6 + len(bufs)),
        scratch_shapes=scratch,
        compiler_params=vmem(16),
        cost_estimate=cost(
            2 * rows * d * width + 6 * seq * d * width + 10 * rows * seq * width,
            8 * d * width + 4 * seq * d + 12 * seq * width,
            rows * seq * width // HEAD,
        ),
    )(q, k, v, gm, segments, slots, *bufs)


def attend_grads_kernel(n0_ref, n1_ref, d0_ref, d1_ref, g0_ref, g1_ref, m0_ref, m1_ref, *outs):
    d = n0_ref.shape[1]
    width = m0_ref.shape[1]
    groups = d // BLOCK
    nt = [n0_ref[...].T, n1_ref[...].T]
    for which in range(3):
        total = dot(nt[0], d0_ref[which]) + dot(nt[1], d1_ref[which])
        store_blocks(
            total.astype(BF).reshape(groups, BLOCK, width),
            outs,
            slice(which * BLOCK, (which + 1) * BLOCK),
        )
    total = dot(g0_ref[...].T, m0_ref[...]) + dot(g1_ref[...].T, m1_ref[...])
    store_blocks(
        total.astype(BF).reshape(groups, BLOCK, width), outs, slice(3 * BLOCK, 4 * BLOCK)
    )


def grad_shapes(count, groups, rows, width, split):
    if split:
        return [shape((count // 2, rows, width), BF)] * 2
    return [shape((groups, rows, width), BF)]


def attend_grads(count, split, n, dj, gm, mixed):
    seq, d = n[0].shape
    width = mixed[0].shape[1]
    outs = grad_shapes(count, d // BLOCK, 4 * BLOCK, width, split)
    return pl.pallas_call(
        attend_grads_kernel,
        name="attend_grads",
        out_shape=outs,
        in_specs=[VMEM] * 8,
        compiler_params=vmem(16),
        cost_estimate=cost(16 * seq * d * width, 16 * d * width + 8 * seq * d),
    )(*n, *dj, *gm, *mixed)


def chunk_of(hidden):
    return 512 if hidden % 512 == 0 else hidden


def mlp_forward_kernel(count, layer, arrays, n0_ref, n1_ref, be_ref, *refs):
    e_bufs, s_bufs = refs[:arrays], refs[arrays : 2 * arrays]
    out0_ref, out1_ref, n_ref, acc_ref, we_ref, ws_ref = refs[2 * arrays :]
    rows, d = n0_ref.shape
    hidden = e_bufs[0].shape[2]
    chunk = chunk_of(hidden)
    n_ref[:rows, :] = n0_ref[...]
    n_ref[rows:, :] = n1_ref[...]
    acc_ref[...] = jnp.zeros_like(acc_ref)

    @pl.loop(0, hidden // chunk)
    def _(index):
        cols = pl.ds(pl.multiple_of(index * chunk, chunk), chunk)
        load_blocks(e_bufs, we_ref, cols)
        load_blocks(s_bufs, ws_ref, cols)
        shift = be_ref[:, cols].astype(F32)[layer : layer + 1, :]
        u = dot(n_ref[...], we_ref[...].reshape(d, chunk)) + shift
        t = jnp.tanh(GELU_C * (u + GELU_A * (u * u * u)))
        active = (0.5 * u * (1.0 + t)).astype(BF)
        acc_ref[...] = acc_ref[...] + dot_nt(active, ws_ref[...].reshape(d, chunk))

    out0_ref[...] = acc_ref[:rows, :].astype(BF)
    out1_ref[...] = acc_ref[rows:, :].astype(BF)


def mlp_forward(count, layer, n, be, e_bufs, s_bufs):
    rows, d = n[0].shape
    hidden = e_bufs[0].shape[-1]
    return pl.pallas_call(
        partial(mlp_forward_kernel, count, layer, len(e_bufs)),
        name="mlp_forward",
        out_shape=[shape((rows, d), BF)] * 2,
        in_specs=[VMEM] * (3 + 2 * len(e_bufs)),
        scratch_shapes=[
            pltpu.VMEM((2 * rows, d), BF),
            pltpu.VMEM((2 * rows, d), F32),
            pltpu.VMEM((d // BLOCK, BLOCK, chunk_of(hidden)), BF),
            pltpu.VMEM((d // BLOCK, BLOCK, chunk_of(hidden)), BF),
        ],
        compiler_params=vmem(16),
        cost_estimate=cost(
            8 * rows * d * hidden, 4 * d * hidden + 8 * rows * d, 2 * rows * hidden
        ),
    )(*n, be, *e_bufs, *s_bufs)


def mlp_backward_kernel(count, layer, arrays, full, outputs, n0_ref, n1_ref, g0_ref, g1_ref, be_ref, *refs):
    e_bufs, s_bufs = refs[:arrays], refs[arrays : 2 * arrays]
    refs = refs[2 * arrays :]
    if full:
        out0_ref, out1_ref, refs = refs[0], refs[1], refs[2:]
    gn0_ref, gn1_ref, gb_ref = refs[:3]
    outs = refs[3 : 3 + outputs]
    refs = refs[3 + outputs :]
    n_ref, g_ref, nt_ref, gt_ref, gacc_ref, we_ref, ws_ref = refs[:7]
    if full:
        acc_ref = refs[7]
    rows, d = n0_ref.shape
    hidden = e_bufs[0].shape[2]
    chunk = chunk_of(hidden)
    groups = d // BLOCK
    n_ref[:rows, :] = n0_ref[...]
    n_ref[rows:, :] = n1_ref[...]
    g_ref[:rows, :] = g0_ref[...]
    g_ref[rows:, :] = g1_ref[...]
    nt_ref[...] = n_ref[...].T
    gt_ref[...] = g_ref[...].T
    gacc_ref[...] = jnp.zeros_like(gacc_ref)
    if full:
        acc_ref[...] = jnp.zeros_like(acc_ref)

    @pl.loop(0, hidden // chunk)
    def _(index):
        cols = pl.ds(pl.multiple_of(index * chunk, chunk), chunk)
        load_blocks(e_bufs, we_ref, cols)
        load_blocks(s_bufs, ws_ref, cols)
        we = we_ref[...].reshape(d, chunk)
        ws = ws_ref[...].reshape(d, chunk)
        shift = be_ref[:, cols].astype(F32)[layer : layer + 1, :]
        u = dot(n_ref[...], we) + shift
        square = u * u
        t = jnp.tanh(GELU_C * (u + GELU_A * (square * u)))
        lean = 0.5 * (1.0 + t)
        active = (u * lean).astype(BF)
        slope = lean + (0.5 * u) * (1.0 - t * t) * (GELU_C + (3.0 * GELU_C * GELU_A) * square)
        gh = dot(g_ref[...], ws) * slope
        gb_ref[:, cols] = jnp.sum(gh, axis=0, keepdims=True)
        gh = gh.astype(BF)
        ge = dot(nt_ref[...], gh).astype(BF)
        gs = dot(gt_ref[...], active).astype(BF)
        store_blocks(ge.reshape(groups, BLOCK, chunk), outs, slice(0, BLOCK), cols)
        store_blocks(gs.reshape(groups, BLOCK, chunk), outs, slice(BLOCK, 2 * BLOCK), cols)
        gacc_ref[...] = gacc_ref[...] + dot_nt(gh, we)
        if full:
            acc_ref[...] = acc_ref[...] + dot_nt(active, ws)

    gn0_ref[...] = gacc_ref[:rows, :].astype(BF)
    gn1_ref[...] = gacc_ref[rows:, :].astype(BF)
    if full:
        out0_ref[...] = acc_ref[:rows, :].astype(BF)
        out1_ref[...] = acc_ref[rows:, :].astype(BF)


def mlp_backward(count, layer, split, n, g, be, e_bufs, s_bufs, full):
    rows, d = n[0].shape
    hidden = e_bufs[0].shape[-1]
    groups = d // BLOCK
    half = shape((rows, d), BF)
    grads = grad_shapes(count, groups, 2 * BLOCK, hidden, split)
    blocks = pltpu.VMEM((groups, BLOCK, chunk_of(hidden)), BF)
    return pl.pallas_call(
        partial(mlp_backward_kernel, count, layer, len(e_bufs), full, len(grads)),
        name="mlp_backward",
        out_shape=[half] * (4 if full else 2) + [shape((1, hidden), F32)] + grads,
        in_specs=[VMEM] * (5 + 2 * len(e_bufs)),
        scratch_shapes=[
            pltpu.VMEM((2 * rows, d), BF),
            pltpu.VMEM((2 * rows, d), BF),
            pltpu.VMEM((d, 2 * rows), BF),
            pltpu.VMEM((d, 2 * rows), BF),
            pltpu.VMEM((2 * rows, d), F32),
            blocks,
            blocks,
        ]
        + ([pltpu.VMEM((2 * rows, d), F32)] if full else []),
        compiler_params=vmem(28),
        cost_estimate=cost(
            (24 if full else 20) * rows * d * hidden,
            8 * d * hidden + 16 * rows * d,
            2 * rows * hidden,
        ),
    )(*n, *g, be, *e_bufs, *s_bufs)


def middle_kernel(layer, x_ref, own_ref, got_ref, slots_ref, gain_ref, shift_ref, bias_ref, *outs):
    middle = (
        x_ref[...].astype(F32)
        + (own_ref[...].astype(F32) + got_ref[...].astype(F32))
        + row_of(bias_ref, layer, 0)
    )
    unit, _ = statistics(middle)
    normed = (unit * row_of(gain_ref, layer, 1) + row_of(shift_ref, layer, 1)).astype(BF)
    outs[0][...] = middle
    outs[1][...] = normed
    if layer == 0:
        hit = ones(place_rows(slots_ref, 1, x_ref.shape[0]))
        outs[2][...] = exact_pick(hit, middle)
        outs[3][...] = dot(hit, normed).astype(BF)


def second_kernel(
    x_ref, mid_ref, own_ref, got_ref, slots_ref, gain_ref, shift_ref, bias_ref, out_ref, n_ref
):
    seq = x_ref.shape[0]
    latent = (
        mid_ref[...]
        + (own_ref[...].astype(F32) + got_ref[...].astype(F32))
        + row_of(bias_ref, 0, 1)
    )
    known = column(slots_ref[...]) >= 1.0
    latent = jnp.where(known, latent, 0.0).astype(BF)
    hit = place_columns(slots_ref, 0, seq)
    occupied = jnp.sum(jnp.where(hit, 1.0, 0.0), axis=-1, keepdims=True)
    second = x_ref[...].astype(F32) * (1.0 - occupied) + dot(ones(hit), latent)
    unit, _ = statistics(second)
    out_ref[...] = second
    n_ref[...] = (unit * row_of(gain_ref, 1, 0) + row_of(shift_ref, 1, 0)).astype(BF)


def grad_middle_kernel(mid_ref, own_ref, got_ref, cot_ref, gain_ref, out_ref, low_ref, sum_ref):
    cot = cot_ref[...].astype(F32)
    grad = own_ref[...].astype(F32) + got_ref[...].astype(F32)
    back, gain, shift = norm_backward(mid_ref[...], grad, row_of(gain_ref, 1, 1))
    total = cot + back
    out_ref[...] = total
    low_ref[...] = total.astype(BF)
    sum_ref[0:1, :] = gain
    sum_ref[1:2, :] = shift
    sum_ref[2:3, :] = jnp.sum(total, axis=0, keepdims=True)
    sum_ref[3:4, :] = jnp.sum(cot, axis=0, keepdims=True)


def grad_second_kernel(
    x_ref, own_ref, got_ref, gm_ref, slots_ref, gain_ref, out_ref, pick_ref, low_ref, sum_ref
):
    grad = own_ref[...].astype(F32) + got_ref[...].astype(F32)
    back, gain, shift = norm_backward(x_ref[...], grad, row_of(gain_ref, 1, 0))
    total = gm_ref[...] + back
    out_ref[...] = total
    hit = place_rows(slots_ref, 0, x_ref.shape[0])
    known = column(slots_ref[...]) >= 1.0
    pick = jnp.where(known, exact_pick(ones(hit), total), 0.0)
    pick_ref[...] = pick
    low_ref[...] = pick.astype(BF)
    sum_ref[0:1, :] = gain
    sum_ref[1:2, :] = shift


def grad_picked_kernel(mid_ref, own_ref, got_ref, pick_ref, gain_ref, out_ref, low_ref, sum_ref):
    grad = own_ref[...].astype(F32) + got_ref[...].astype(F32)
    back, gain, shift = norm_backward(mid_ref[...], grad, row_of(gain_ref, 0, 1))
    pick = pick_ref[...]
    total = pick + back
    out_ref[...] = total
    low_ref[...] = total.astype(BF)
    sum_ref[0:1, :] = gain
    sum_ref[1:2, :] = shift
    sum_ref[2:3, :] = jnp.sum(total, axis=0, keepdims=True)
    sum_ref[3:4, :] = jnp.sum(pick, axis=0, keepdims=True)


def grad_first_kernel(
    x_ref, own_ref, got_ref, gm_ref, second_ref, slots_ref, gain_ref,
    s22_ref, s21_ref, s12_ref, pair1_ref, pair0_ref, peer1_ref, peer0_ref, be1_ref, be0_ref,
    out_ref, sum_ref,
):
    seq, d = x_ref.shape
    grad = own_ref[...].astype(F32) + got_ref[...].astype(F32)
    back, gain, shift = norm_backward(x_ref[...].astype(F32), grad, row_of(gain_ref, 0, 0))
    hit = place_columns(slots_ref, 0, seq)
    occupied = jnp.sum(jnp.where(hit, 1.0, 0.0), axis=-1, keepdims=True)
    source = ones(place_columns(slots_ref, 1, seq))
    out_ref[...] = second_ref[...] * (1.0 - occupied) + (exact_pick(source, gm_ref[...]) + back)
    width = pair0_ref.shape[1]
    for index, row in enumerate(
        (
            gain, s12_ref[0:1, :], s21_ref[0:1, :], s22_ref[0:1, :],
            shift, s12_ref[1:2, :], s21_ref[1:2, :], s22_ref[1:2, :],
            s12_ref[2:3, :], s12_ref[3:4, :], s22_ref[2:3, :], s22_ref[3:4, :],
        )
    ):
        for part in range(d // width):
            at = index * (d // width) + part
            sum_ref[at : at + 1, :] = row[:, part * width : (part + 1) * width]
    first = 12 * (d // width)
    sum_ref[first : first + 2, :] = pair0_ref[...] + peer0_ref[...]
    sum_ref[first + 2 : first + 4, :] = pair1_ref[...] + peer1_ref[...]
    hidden = be0_ref.shape[1]
    for layer, ref in enumerate((be0_ref, be1_ref)):
        for part in range(hidden // width):
            at = first + 4 + layer * (hidden // width) + part
            sum_ref[at : at + 1, :] = ref[0:1, part * width : (part + 1) * width]


def vectors_kernel(sum_ref, gains_ref, shifts_ref, branch_ref, pair_ref, hidden_ref):
    d = gains_ref.shape[2]
    width = sum_ref.shape[1]
    index = 0
    for ref in (gains_ref, shifts_ref, branch_ref):
        for layer in range(2):
            for which in range(2):
                for part in range(d // width):
                    ref[layer, which : which + 1, part * width : (part + 1) * width] = sum_ref[
                        index : index + 1, :
                    ]
                    index += 1
    for layer in range(2):
        pair_ref[layer] = sum_ref[index : index + 2, :]
        index += 2
    for layer in range(2):
        for part in range(hidden_ref.shape[1] // width):
            hidden_ref[layer : layer + 1, part * width : (part + 1) * width] = sum_ref[
                index : index + 1, :
            ]
            index += 1


def small(kernel, name, outs, *args):
    moved = sum(a.size * a.dtype.itemsize for a in args) + sum(
        o.size * o.dtype.itemsize for o in outs
    )
    return pl.pallas_call(
        kernel,
        name=name,
        out_shape=outs,
        in_specs=[VMEM] * len(args),
        compiler_params=vmem(24),
        cost_estimate=cost(4 * moved, moved),
    )(*args)


def split_kernel(stride, keep_ref, got_ref, kept_ref, sent_ref):
    bit = lax.rem(lax.axis_index("fsdp") // stride, 2)
    for index in range(kept_ref.shape[0]):
        for out, place in ((kept_ref, bit), (sent_ref, 1 - bit)):
            at = 2 * index + place
            out[index] = (keep_ref[at].astype(F32) + got_ref[at].astype(F32)).astype(BF)


def split(keep, got, stride):
    blocks, rows, width = keep.shape
    return pl.pallas_call(
        partial(split_kernel, stride),
        name="split",
        out_shape=[shape((blocks // 2, rows, width), BF)] * 2,
        in_specs=[VMEM] * 2,
        compiler_params=vmem(8),
        cost_estimate=cost(keep.size, 6 * keep.size),
    )(keep, got)


def finish_kernel(kinds, *refs):
    outs = refs[-len(kinds) :]
    each = (len(refs) - len(outs)) // 2
    for layer in range(2):
        parts = refs[layer * each : (layer + 1) * each]
        total = parts[0][0].astype(F32)
        for part in parts[1:]:
            total = total + part[0].astype(F32)
        rows = total.shape[0] // sum(kinds)
        first = 0
        for kind, out in zip(kinds, outs):
            for which in range(kind):
                piece = total[first : first + rows, :]
                if kind == 1:
                    out[layer] = piece
                else:
                    out[layer, which] = piece
                first += rows


def finish(kinds, *states):
    _, rows, width = states[0][0].shape
    each = rows // sum(kinds)
    outs = [
        shape((2, each, width) if kind == 1 else (2, kind, each, width), F32) for kind in kinds
    ]
    return small(partial(finish_kernel, kinds), "finish", outs, *states[0], *states[1])


def sum_everywhere(value, count):
    stride = 1
    while stride < count and count % (2 * stride) == 0:
        pairs = [(source, source ^ stride) for source in range(count)]
        value = value + lax.ppermute(value, "fsdp", pairs)
        stride *= 2
    if stride < count:
        groups = [list(range(first, count, stride)) for first in range(stride)]
        value = lax.psum(value, "fsdp", axis_index_groups=groups)
    return value


def regroup(array, count, kinds):
    rows = array.shape[0] * array.shape[1] // kinds // BLOCK
    each = array.shape[1] // kinds
    width = array.shape[2]
    split = array.reshape(array.shape[0], kinds, each, width).transpose(1, 0, 2, 3)
    return split.reshape(kinds, rows, BLOCK, width).transpose(1, 0, 2, 3).reshape(
        rows, kinds * BLOCK, width
    )


def ungroup(array, count, kinds):
    width = array.shape[2]
    split = array.reshape(array.shape[0], kinds, BLOCK, width).transpose(1, 0, 2, 3)
    each = array.shape[0] * BLOCK // count
    return split.reshape(kinds, count, each, width).transpose(1, 0, 2, 3).reshape(
        count, kinds * each, width
    )


def shards(
    count,
    embedded,
    segments,
    thoughts,
    cotangent,
    gains,
    shifts,
    joint_weight,
    joint_bias,
    merge_weight,
    expand_weight,
    expand_bias,
    shrink_weight,
    branch_biases,
):
    seq, d = embedded.shape
    rows_each = joint_weight.shape[1]
    width = joint_weight.shape[3]
    hidden = expand_weight.shape[2]
    slots = thoughts.shape[1]
    staged = rows_each == BLOCK and count == 16
    rows_f32, rows_bf = shape((seq, d), F32), shape((seq, d), BF)
    few_f32, few_bf = shape((slots, d), F32), shape((slots, d), BF)
    ins = (
        joint_weight.transpose(0, 2, 1, 3),
        merge_weight.transpose(0, 2, 1),
        expand_weight,
        shrink_weight.transpose(0, 2, 1),
    )
    shard, parts, joined, bufs = {}, {}, {}, {}

    def fetch(name, *others):
        if staged:
            own = after(shard[name], *others)
            parts[name] = join(own, across(own, count, 8))
        return parts.get(name, ())

    def further(name, *others):
        if staged:
            own = after(parts[name], *others)
            joined[name] = join(own, across(own, count, 4))
        return joined.get(name, ())

    def arrive(name, *others):
        if staged:
            own = after(joined[name], *others)
            got = across(own, count, 2)
            bufs[name] = [own, got, across(own, count, 1), across(got, count, 1)]

    if staged:
        shard["a0"], normed = start(*ins[:2], embedded, gains, shifts)
        for name, one in zip(("e0", "s0", "a1", "e1", "s1"), rest(*ins)):
            shard[name] = one
    else:
        first = embedded.astype(F32)
        center = first - jnp.mean(first, axis=-1, keepdims=True)
        scale = lax.rsqrt(jnp.mean(center * center, axis=-1, keepdims=True) + EPSILON)
        normed = (
            center * scale * gains[0, 0].astype(F32) + shifts[0, 0].astype(F32)
        ).astype(BF)
        for layer in range(2):
            attend = jnp.concatenate(
                (ins[0][layer].reshape(3 * rows_each, width), ins[1][layer]), axis=0
            )
            for name, one, kind in (("a", attend, 4), ("e", ins[2][layer], 1), ("s", ins[3][layer], 1)):
                whole = lax.all_gather(one, "fsdp", axis=0, tiled=False)
                bufs[f"{name}{layer}"] = [regroup(whole, count, kind)]

    slots_peer = swap(thoughts)
    normed_peer = swap(normed)
    cot_peer = swap(after(cotangent, normed_peer))

    def attention(layer, own, peer, *others):
        weights = bufs[f"a{layer}"]
        part_peer, *kept_peer = attend_forward(count, layer, True, peer, segments, joint_bias, weights)
        got = swap(part_peer)
        part_own, *kept_own = attend_forward(
            count, layer, False, after(own, part_peer, *others), segments, joint_bias, weights
        )
        return (part_own, got, (own, peer), (kept_own, kept_peer))

    here = fetch("a0")
    here = fetch("e0", here)
    further("a0", shard.get("e0", ()))
    arrive("a0")
    ready = further("e0")
    here = fetch("s0", here)
    part, got, n_one, kept_one = attention(0, normed, after(normed_peer, ready), here)
    arrive("e0")
    ready = further("s0")
    here = fetch("a1", here)
    middle_one, n2_one, middle_few, n2_few = small(
        partial(middle_kernel, 0), "middle", [rows_f32, rows_bf, few_f32, few_bf],
        embedded, after(part, ready), got, thoughts, gains, shifts, branch_biases,
    )
    n2_few = (n2_few, swap(n2_few))
    n2_all = (n2_one, swap(after(n2_one, n2_few[1])))
    arrive("s0")
    ready = further("a1")
    here = fetch("e1", here)
    own, peer = mlp_forward(count, 0, after(n2_few, ready), expand_bias, bufs["e0"], bufs["s0"])
    second, normed = small(
        second_kernel, "second", [rows_f32, rows_bf],
        embedded, middle_few, after(own, here), swap(peer), thoughts, gains, shifts, branch_biases,
    )

    arrive("a1")
    ready = further("e1")
    here = fetch("s1", here)
    part, got, n_two, kept_two = attention(1, normed, after(swap(normed), ready, here))
    arrive("e1")
    ready = further("s1")
    middle_two, n2_two = small(
        partial(middle_kernel, 1), "middle", [rows_f32, rows_bf],
        second, after(part, ready), got, thoughts, gains, shifts, branch_biases,
    )
    arrive("s1")
    n2_peer = swap(n2_two)
    latent_own, latent_peer = mlp_forward(
        count, 0, after(n2_all, n2_two), expand_bias, bufs["e0"], bufs["s0"]
    )
    own_two, peer_two, gn_own, gn_peer, gb_two, *m1 = mlp_backward(
        count, 1, staged, (n2_two, after(n2_peer, latent_own)), (cotangent, cot_peer),
        expand_bias, bufs["e1"], bufs["s1"], True,
    )
    latent_got = swap(after(latent_peer, n2_peer))

    def core_step(grads, kind):
        if staged:
            return (grads[0], across(grads[1], count, 1))
        done = lax.psum_scatter(
            ungroup(grads[0], count, kind), "fsdp", scatter_dimension=0, tiled=False
        )
        return (done[None],)

    def send(state, stride):
        return split(*state, stride) if staged else state

    def move(state, stride):
        return (state[0], across(state[1], count, stride)) if staged else state

    got = swap(gn_peer)
    m1 = core_step(m1, 2)
    gm, gm_low, s22 = small(
        grad_middle_kernel, "grad_middle", [rows_f32, rows_bf, shape((4, d), F32)],
        middle_two, after(gn_own, m1), got, cotangent, gains,
    )
    gm_peer = swap(gm_low)
    m1 = send(m1, 2)
    weights = bufs["a1"]
    back_peer = attend_backward(
        count, 1, True, kept_two[1][:3], after(gm_peer, m1), segments, slots_peer, weights, False
    )
    m1 = move(m1, 2)
    got = swap(back_peer[0])
    back_own = attend_backward(
        count, 1, False, kept_two[0][:3], after(gm_low, back_peer[0]), segments, thoughts, weights, False
    )
    a1 = attend_grads(
        count, staged, n_two, (back_own[1], back_peer[1]), (gm_low, gm_peer),
        (kept_two[0][3], kept_two[1][3]),
    )
    grad_second, g_few, g_low, s21 = small(
        grad_second_kernel, "grad_second", [rows_f32, few_f32, few_bf, shape((2, d), F32)],
        second, after(back_own[0], a1), got, gm, thoughts, gains,
    )
    pair_two = (back_own[2], back_peer[2])
    a1 = core_step(a1, 4)
    m1 = send(m1, 4)

    own, peer, gb_one, *m0 = mlp_backward(
        count, 0, staged, n2_few, (g_low, after(swap(g_low), m1, a1)), expand_bias,
        bufs["e0"], bufs["s0"], False,
    )
    m1 = move(m1, 4)
    a1 = send(a1, 2)
    m0 = core_step(m0, 2)
    gm_few, gm_low, s12 = small(
        grad_picked_kernel, "grad_picked", [few_f32, few_bf, shape((4, d), F32)],
        middle_few, after(own, a1), swap(peer), g_few, gains,
    )
    a1 = move(a1, 2)
    m0 = send(m0, 2)
    m1 = send(m1, 8)
    weights = bufs["a0"]
    back_peer = attend_backward(
        count, 0, True, kept_one[1][:3], after(swap(gm_low), m0, m1), segments, slots_peer, weights, True
    )
    m1 = move(m1, 8)
    m0 = move(m0, 2)
    got = swap(back_peer[0])
    back_own = attend_backward(
        count, 0, False, kept_one[0][:3], after(gm_low, back_peer[0]), segments, thoughts, weights, True
    )
    a1 = send(a1, 4)
    a0 = attend_grads(
        count, staged, n_one, (after(back_own[1], a1), back_peer[1]), (back_own[3], back_peer[3]),
        (kept_one[0][3], kept_one[1][3]),
    )
    a1 = move(a1, 4)
    pair_one = (back_own[2], back_peer[2])
    a0 = core_step(a0, 4)
    embedded_grad, vectors = small(
        grad_first_kernel, "grad_first",
        [rows_f32, shape((12 * d // width + 4 + 2 * (hidden // width), width), F32)],
        embedded, back_own[0], got, gm_few, grad_second, thoughts, gains,
        s22, s21, s12, pair_two[0], pair_one[0], pair_two[1], pair_one[1], gb_two, gb_one,
    )
    a1 = move(send(a1, 8), 8)
    a0 = move(send(a0, 2), 2)
    m0 = move(send(m0, 4), 4)
    m0 = move(send(m0, 8), 8)
    a0 = move(send(a0, 4), 4)
    a0 = move(send(a0, 8), 8)

    biases = branch_biases.astype(F32)
    latent = middle_one + (latent_own.astype(F32) + latent_got.astype(F32)) + biases[0, 1]
    language = middle_two + (own_two.astype(F32) + swap(peer_two).astype(F32)) + biases[1, 1]

    joint_grad, merge_grad = finish((3, 1), a0, a1)
    expand_grad, shrink_grad = finish((1, 1), m0, m1)
    shared = jnp.arange(vectors.shape[0])[:, None] < 12 * d // width
    total = sum_everywhere(vectors + jnp.where(shared, swap(vectors), 0.0), count)
    vector = shape((2, 2, d), F32)
    gains_grad, shifts_grad, branch_grad, joint_bias_grad, expand_bias_grad = small(
        vectors_kernel, "vectors",
        [vector, vector, vector, shape((2, 2, width), F32), shape((2, hidden), F32)], total,
    )
    return (
        latent.astype(BF),
        language.astype(BF),
        embedded_grad,
        gains_grad,
        shifts_grad,
        joint_grad.transpose(0, 2, 1, 3),
        joint_bias_grad,
        merge_grad.transpose(0, 2, 1),
        expand_grad,
        expand_bias_grad,
        shrink_grad.transpose(0, 2, 1),
        branch_grad,
    )


def solution(mesh):
    placed = (
        P(("fsdp", "tensor"), None),
        P("fsdp", None),
        P(("fsdp", "tensor"), None),
        P(("fsdp", "tensor"), None),
        P(),
        P(),
        P(None, "fsdp", None, "tensor"),
        P(None, None, "tensor"),
        P(None, "tensor", "fsdp"),
        P(None, "fsdp", "tensor"),
        P(None, "tensor"),
        P(None, "tensor", "fsdp"),
        P(),
    )
    return jax.shard_map(
        partial(shards, mesh.shape["fsdp"]),
        mesh=mesh,
        in_specs=placed,
        out_specs=(
            P(("fsdp", "tensor"), None),
            P(("fsdp", "tensor"), None),
            P(("fsdp", "tensor"), None),
            P(),
            P(),
            P(None, "fsdp", None, "tensor"),
            P(None, None, "tensor"),
            P(None, "tensor", "fsdp"),
            P(None, "fsdp", "tensor"),
            P(None, "tensor"),
            P(None, "tensor", "fsdp"),
            P(),
        ),
        check_vma=False,
    )
```

time: 1240 us -> 362 us (0.29)
  waiting for transfers between devices: 680 us -> 188 us
  blocking collectives: 247 us -> 0 us
  matrix products: 123 us -> 0 us
  local copies, waits for them, and re-layouts: 88.3 us -> 6.19 us
  starting transfers between devices: 1.16 us -> 82.9 us
  Pallas kernels: 0 us -> 74.7 us
  other arithmetic: 58.2 us -> 1.91 us
  between operations: 16 us -> 1.46 us
  loops' own time: 13.3 us -> 0 us
    reduce_scatter x16 -> x0, waiting for transfers between devices: 512 us -> none  [the longest x2 156 us: reduce_weights(): lax.psum_scatter(matrices[2], 'fsdp', scatter_dimension=0, tiled=True)]
    ppermute x0 -> x70, waiting for transfers between devices: none -> 188 us  [the longest x46 104 us: across(): lax.ppermute(value, 'fsdp', [(place, place ^ stride) for place in range(c...]
    all_gather x6 -> x0, waiting for transfers between devices: 166 us -> none  [the longest x2 78.6 us: fetch_weights(): lax.all_gather(shrink, 'fsdp', axis=1, tiled=True)]
    all_gather x10 -> x0, blocking collectives: 148 us -> none  [the longest x8 103 us: gather_rows(): return lax.all_gather(rows, 'tensor', axis=0, tiled=True)]
    dot_general x55 -> x0, matrix products: 123 us -> none  [the longest x8 25.9 us: scatter_rows(): jnp.einsum(pattern, source, weight, preferred_element_type=jnp.float32)]
    psum x2 -> x0, blocking collectives: 98.6 us -> none  [the longest x1 60.4 us: shards(): lax.psum((jnp.stack((split_one[0], split_two[0])), jnp.stack((split_one[1...]
    ppermute x0 -> x70, starting transfers between devices: none -> 82.9 us  [the longest x46 49.5 us: across(): lax.ppermute(value, 'fsdp', [(place, place ^ stride) for place in range(c...]
    pallas_call x0 -> x50, Pallas kernels: none -> 74.7 us  [the longest x4 22.4 us: attend_backward(): pl.pallas_call(partial(attend_backward_kernel, count, layer, peer, picked...]
  transfers between devices with their start and end apart: 22 -> 70, of which waited for: 18 -> 34; matrix products, arithmetic and copies ran while one was open for 7% -> 1% of each run, Pallas kernels for 0% -> 14%
where the time goes in v2:
time: 362 us; the launch traced here: 355 us
  waiting for transfers between devices  188 us (52%)
  starting transfers between devices  82.9 us (23%)
  Pallas kernels  74.7 us (21%)
  local copies, waits for them, and re-layouts  6.19 us (2%)
    ppermute x46, waiting for transfers between devices, across(): lax.ppermute(value, 'fsdp', [(place, place ^ stride) for place in range(c...  104 us
    ppermute x46, starting transfers between devices, across(): lax.ppermute(value, 'fsdp', [(place, place ^ stride) for place in range(c...  49.5 us
    ppermute x20, waiting for transfers between devices, swap(): return lax.ppermute(value, 'tensor', [(0, 1), (1, 0)])  46.9 us
    ppermute x4, waiting for transfers between devices, sum_everywhere(): value = value + lax.ppermute(value, 'fsdp', pairs)  36.9 us
    ppermute x20, starting transfers between devices, swap(): return lax.ppermute(value, 'tensor', [(0, 1), (1, 0)])  28.3 us
    pallas_call x4, Pallas kernels, attend_backward(): pl.pallas_call(partial(attend_backward_kernel, count, layer, peer, picked...  22.4 us
    pallas_call x4, Pallas kernels, attend_forward(): pl.pallas_call(partial(attend_forward_kernel, count, layer, peer, len(buf...  15.4 us
    pallas_call x2, Pallas kernels, mlp_backward(): pl.pallas_call(partial(mlp_backward_kernel, count, layer, len(e_bufs), fu...  13.9 us
  transfers between devices with their start and end apart: 70, of which 34 were waited for; matrix products, arithmetic and copies ran while one was open for 1% of the time, Pallas kernels for 14%

profile of v2, /device:TPU:0, one launch (start us, length us, event | category | flops | bytes accessed | tf_op | source)
XLA Modules:
  0.0 355.3 jit_solution(8905259748399902556)
XLA Ops:
  5.6 4.1 %collective-permute-start.1 = (bf16[192,384]{1,0:T(8,128)(2,1)S(1)}, bf16[192,384]{1,0:T(8,128)(2,1)S(1)}, u32[]{:S(2)}, u32[]{:S(2)}) collective-permute-start(bf16[192,384]{1,0:T(8,128)(2,1)S(1)} %get-tuple-element.158.own_ref), channel_id=1, source_target_pairs={{0,16},{2,18},{4,20},{6,22},{8,24},{10,26},{12,28},{14,30},{16,0},... | collective-permute-start | bytes 442376 | tf_op jit(solution)/shard_map/ppermute | solution.py:49
  12.6 4.1 %collective-permute-done.1.got_ref = bf16[192,384]{1,0:T(8,128)(2,1)S(1)} collective-permute-done((bf16[192,384]{1,0:T(8,128)(2,1)S(1)}, bf16[192,384]{1,0:T(8,128)(2,1)S(1)}, u32[]{:S(2)}, u32[]{:S(2)}) %collective-permute-start.1) | collective-permute-done | bytes 147488 | tf_op jit(solution)/shard_map/ppermute | solution.py:49
  17.5 7.5 %collective-permute-done.4.got_ref = bf16[2,192,384]{2,1,0:T(8,128)(2,1)S(1)} collective-permute-done((bf16[2,192,384]{2,1,0:T(8,128)(2,1)S(1)}, bf16[2,192,384]{2,1,0:T(8,128)(2,1)S(1)}, u32[]{:S(2)}, u32[]{:S(2)}) %collective-permute-start.4) | collective-permute-done | bytes 294944 | tf_op jit(solution)/shard_map/ppermute | solution.py:49
  29.7 9.0 %collective-permute-done.5.refs_1_ = bf16[4,192,384]{2,1,0:T(8,128)(2,1)S(1)} collective-permute-done((bf16[4,192,384]{2,1,0:T(8,128)(2,1)S(1)}, bf16[4,192,384]{2,1,0:T(8,128)(2,1)S(1)}, u32[]{:S(2)}, u32[]{:S(2)}) %collective-permute-start.5) | collective-permute-done | bytes 589856 | tf_op jit(solution)/shard_map/ppermute | solution.py:49
  38.7 4.3 %collective-permute-start.8 = (bf16[48,1536]{1,0:T(8,128)(2,1)S(1)}, bf16[48,1536]{1,0:T(8,128)(2,1)S(1)}, u32[]{:S(2)}, u32[]{:S(2)}) collective-permute-start(bf16[48,1536]{1,0:T(8,128)(2,1)S(1)} %get-tuple-element.164.own_ref), channel_id=1, source_target_pairs={{0,16},{2,18},{4,20},{6,22},{8,24},{10,26},{12,28},{14,30},{16,0},... | collective-permute-start | bytes 442376 | tf_op jit(solution)/shard_map/ppermute | solution.py:49
  44.4 6.4 %collective-permute-done.8.got_ref = bf16[48,1536]{1,0:T(8,128)(2,1)S(1)} collective-permute-done((bf16[48,1536]{1,0:T(8,128)(2,1)S(1)}, bf16[48,1536]{1,0:T(8,128)(2,1)S(1)}, u32[]{:S(2)}, u32[]{:S(2)}) %collective-permute-start.8) | collective-permute-done | bytes 147488 | tf_op jit(solution)/shard_map/ppermute | solution.py:49
  56.7 4.0 %collective-permute-done.9.got_ref = bf16[2,48,1536]{2,1,0:T(8,128)(2,1)S(1)} collective-permute-done((bf16[2,48,1536]{2,1,0:T(8,128)(2,1)S(1)}, bf16[2,48,1536]{2,1,0:T(8,128)(2,1)S(1)}, u32[]{:S(2)}, u32[]{:S(2)}) %collective-permute-start.9) | collective-permute-done | bytes 294944 | tf_op jit(solution)/shard_map/ppermute | solution.py:49
  71.7 8.0 %collective-permute-done.14.got_ref = bf16[2,192,384]{2,1,0:T(8,128)(2,1)S(1)} collective-permute-done((bf16[2,192,384]{2,1,0:T(8,128)(2,1)S(1)}, bf16[2,192,384]{2,1,0:T(8,128)(2,1)S(1)}, u32[]{:S(2)}, u32[]{:S(2)}) %collective-permute-start.14) | collective-permute-done | bytes 294944 | tf_op jit(solution)/shard_map/ppermute | solution.py:49
  88.7 5.7 %collective-permute-done.26.refs_1_ = bf16[4,192,384]{2,1,0:T(8,128)(2,1)S(1)} collective-permute-done((bf16[4,192,384]{2,1,0:T(8,128)(2,1)S(1)}, bf16[4,192,384]{2,1,0:T(8,128)(2,1)S(1)}, u32[]{:S(2)}, u32[]{:S(2)}) %collective-permute-start.26) | collective-permute-done | bytes 589856 | tf_op jit(solution)/shard_map/ppermute | solution.py:49
  100.2 4.6 %collective-permute-done.21.got_ref = bf16[48,1536]{1,0:T(8,128)(2,1)S(1)} collective-permute-done((bf16[48,1536]{1,0:T(8,128)(2,1)S(1)}, bf16[48,1536]{1,0:T(8,128)(2,1)S(1)}, u32[]{:S(2)}, u32[]{:S(2)}) %collective-permute-start.21) | collective-permute-done | bytes 147488 | tf_op jit(solution)/shard_map/ppermute | solution.py:49
  109.9 5.9 %collective-permute-done.25.got_ref = bf16[48,1536]{1,0:T(8,128)(2,1)S(1)} collective-permute-done((bf16[48,1536]{1,0:T(8,128)(2,1)S(1)}, bf16[48,1536]{1,0:T(8,128)(2,1)S(1)}, u32[]{:S(2)}, u32[]{:S(2)}) %collective-permute-start.25) | collective-permute-done | bytes 147488 | tf_op jit(solution)/shard_map/ppermute | solution.py:49
  116.0 4.4 %collective-permute-done.24.got_ref = bf16[2,48,1536]{2,1,0:T(8,128)(2,1)S(1)} collective-permute-done((bf16[2,48,1536]{2,1,0:T(8,128)(2,1)S(1)}, bf16[2,48,1536]{2,1,0:T(8,128)(2,1)S(1)}, u32[]{:S(2)}, u32[]{:S(2)}) %collective-permute-start.24) | collective-permute-done | bytes 294944 | tf_op jit(solution)/shard_map/ppermute | solution.py:49
  132.3 4.0 %collective-permute-done.30.got_ref = bf16[256,768]{1,0:T(8,128)(2,1)S(1)} collective-permute-done((bf16[256,768]{1,0:T(8,128)(2,1)S(1)}, bf16[256,768]{1,0:T(8,128)(2,1)S(1)}, u32[]{:S(2)}, u32[]{:S(2)}) %collective-permute-start.30) | collective-permute-done | bytes 393248 | tf_op jit(solution)/shard_map/ppermute | solution.py:53
  140.8 9.0 %collective-permute-done.37.refs_5_ = bf16[4,48,1536]{2,1,0:T(8,128)(2,1)S(1)} collective-permute-done((bf16[4,48,1536]{2,1,0:T(8,128)(2,1)S(1)}, bf16[4,48,1536]{2,1,0:T(8,128)(2,1)S(1)}, u32[]{:S(2)}, u32[]{:S(2)}) %collective-permute-start.37) | collective-permute-done | bytes 589856 | tf_op jit(solution)/shard_map/ppermute | solution.py:49
  152.1 3.9 %mlp_forward.3 = (bf16[256,768]{1,0:T(8,128)(2,1)S(1)}, bf16[256,768]{1,0:T(8,128)(2,1)S(1)}) custom-call(bf16[256,768]{1,0:T(8,128)(2,1)S(1)} %get-tuple-element.192.n0_ref, bf16[256,768]{1,0:T(8,128)(2,1)S(1)} %collective-permute-done.12.n1_ref, bf16[2,1536]{1,0:T(2,128)(2,1)S(1)} %copy-done.15, bf16[4,48,1536]{2,1,0:T(8,128)(2,1)S(1)} %join.14.refs_0_, ...), custom_call_target="tpu_custom_call" | custom-call | flops 2415919104 | bytes 6291456 | tf_op jit(solution)/shard_map/mlp_forward/pallas_call | solution.py:490
  156.0 5.5 %collective-permute-done.33.g1_ref = bf16[256,768]{1,0:T(8,128)(2,1)S(1)} collective-permute-done((bf16[256,768]{1,0:T(8,128)(2,1)S(1)}, bf16[256,768]{1,0:T(8,128)(2,1)S(1)}, u32[]{:S(2)}, u32[]{:S(2)}) %collective-permute-start.33) | collective-permute-done | bytes 393248 | tf_op jit(solution)/shard_map/ppermute | solution.py:53
  161.5 9.8 %mlp_backward.2 = (bf16[256,768]{1,0:T(8,128)(2,1)S(1)}, bf16[256,768]{1,0:T(8,128)(2,1)S(1)}, bf16[256,768]{1,0:T(8,128)(2,1)S(1)}, bf16[256,768]{1,0:T(8,128)(...) custom-call(bf16[256,768]{1,0:T(8,128)(2,1)S(1)} %get-tuple-element.191.n0_ref, ...), custom_call_target="tpu_custom_call" | custom-call | flops 7247757312 | bytes 12582912 | tf_op jit(solution)/shard_map/mlp_backward/pallas_call | solution.py:572
  176.0 7.0 %collective-permute-done.42.got_ref = bf16[256,768]{1,0:T(8,128)(2,1)S(1)} collective-permute-done((bf16[256,768]{1,0:T(8,128)(2,1)S(1)}, bf16[256,768]{1,0:T(8,128)(2,1)S(1)}, u32[]{:S(2)}, u32[]{:S(2)}) %collective-permute-start.42) | collective-permute-done | bytes 393248 | tf_op jit(solution)/shard_map/ppermute | solution.py:53
  188.0 6.5 %collective-permute-done.43.gm_ref.g1_ref = bf16[256,768]{1,0:T(8,128)(2,1)S(1)} collective-permute-done((bf16[256,768]{1,0:T(8,128)(2,1)S(1)}, bf16[256,768]{1,0:T(8,128)(2,1)S(1)}, u32[]{:S(2)}, u32[]{:S(2)}) %collective-permute-start.43) | collective-permute-done | bytes 393248 | tf_op jit(solution)/shard_map/ppermute | solution.py:53
  194.5 7.1 %attend_backward.4 = (bf16[256,768]{1,0:T(8,128)(2,1)S(1)}, bf16[3,256,384]{2,1,0:T(8,128)(2,1)S(1)}, f32[2,384]{1,0:T(2,128)S(1)}) custom-call(bf16[256,384]{1,0:T(8,128)(2,1)S(1)} %get-tuple-element.214.q_ref, bf16[256,384]{1,0:T(8,128)(2,1)S(1)} %get-tuple-element.215.k_ref, bf16[256,384]{1,0:T(8,128)(2,1)S(1)} %get-tuple-element.216.v_ref, ...), custom_call_target="tpu_custom_call" | custom-call | flops 855638016 | bytes 4325376 | tf_op jit(solution)/shard_map/attend_backward/pallas_call | solution.py:405
  201.7 7.1 %attend_backward.5 = (bf16[256,768]{1,0:T(8,128)(2,1)S(1)}, bf16[3,256,384]{2,1,0:T(8,128)(2,1)S(1)}, f32[2,384]{1,0:T(2,128)S(1)}) custom-call(bf16[256,384]{1,0:T(8,128)(2,1)S(1)} %get-tuple-element.205.q_ref, bf16[256,384]{1,0:T(8,128)(2,1)S(1)} %get-tuple-element.206.k_ref, bf16[256,384]{1,0:T(8,128)(2,1)S(1)} %get-tuple-element.207.v_ref, ...), custom_call_target="tpu_custom_call" | custom-call | flops 855638016 | bytes 4325376 | tf_op jit(solution)/shard_map/attend_backward/pallas_call | solution.py:405
  212.4 9.8 %collective-permute-done.45.got_ref = bf16[256,768]{1,0:T(8,128)(2,1)S(1)} collective-permute-done((bf16[256,768]{1,0:T(8,128)(2,1)S(1)}, bf16[256,768]{1,0:T(8,128)(2,1)S(1)}, u32[]{:S(2)}, u32[]{:S(2)}) %collective-permute-start.45) | collective-permute-done | bytes 393248 | tf_op jit(solution)/shard_map/ppermute | solution.py:53
  228.0 4.1 %mlp_backward.3 = (bf16[64,768]{1,0:T(8,128)(2,1)S(1)}, bf16[64,768]{1,0:T(8,128)(2,1)S(1)}, f32[1,1536]{1,0:T(1,128)S(1)}, bf16[8,96,1536]{2,1,0:T(8,128)(2,1)S(1)}, bf16[8,96,1536]{2,1,0:T(8,128)(2,1)S(1)}) custom-call(bf16[64,768]{1,0:T(8,128)(2,1)S(1)} %get-tuple-element.175.n0_ref, bf16[64,768]{1,0:T(8,128)(2,1)S(1)} %collective-permute-done.11.n1_ref, ...), custom_call_target="tpu_custom_call" | custom-call | flops 1509949440 | bytes 10223616 | tf_op jit(solution)/shard_map/mlp_backward/pallas_call | solution.py:572
  241.0 6.9 %collective-permute-done.52.got_ref = bf16[2,96,1536]{2,1,0:T(8,128)(2,1)S(1)} collective-permute-done((bf16[2,96,1536]{2,1,0:T(8,128)(2,1)S(1)}, bf16[2,96,1536]{2,1,0:T(8,128)(2,1)S(1)}, u32[]{:S(2)}, u32[]{:S(2)}) %collective-permute-start.52) | collective-permute-done | bytes 589856 | tf_op jit(solution)/shard_map/ppermute | solution.py:49
  248.9 4.1 %attend_backward.6 = (bf16[256,768]{1,0:T(8,128)(2,1)S(1)}, bf16[3,256,384]{2,1,0:T(8,128)(2,1)S(1)}, f32[2,384]{1,0:T(2,128)S(1)}, bf16[256,768]{1,0:T(8,128)(2,1)S(1)}) custom-call(bf16[256,384]{1,0:T(8,128)(2,1)S(1)} %get-tuple-element.242.q_ref, bf16[256,384]{1,0:T(8,128)(2,1)S(1)} %get-tuple-element.243.k_ref, ...), custom_call_target="tpu_custom_call" | custom-call | flops 553648128 | bytes 4325376 | tf_op jit(solution)/shard_map/attend_backward/pallas_call | solution.py:405
  253.0 4.1 %attend_backward.7 = (bf16[256,768]{1,0:T(8,128)(2,1)S(1)}, bf16[3,256,384]{2,1,0:T(8,128)(2,1)S(1)}, f32[2,384]{1,0:T(2,128)S(1)}, bf16[256,768]{1,0:T(8,128)(2,1)S(1)}) custom-call(bf16[256,384]{1,0:T(8,128)(2,1)S(1)} %get-tuple-element.202.q_ref, bf16[256,384]{1,0:T(8,128)(2,1)S(1)} %get-tuple-element.203.k_ref, ...), custom_call_target="tpu_custom_call" | custom-call | flops 553648128 | bytes 4325376 | tf_op jit(solution)/shard_map/attend_backward/pallas_call | solution.py:405
  263.8 8.1 %collective-permute-done.53.got_ref = bf16[256,768]{1,0:T(8,128)(2,1)S(1)} collective-permute-done((bf16[256,768]{1,0:T(8,128)(2,1)S(1)}, bf16[256,768]{1,0:T(8,128)(2,1)S(1)}, u32[]{:S(2)}, u32[]{:S(2)}) %collective-permute-start.53) | collective-permute-done | bytes 393248 | tf_op jit(solution)/shard_map/ppermute | solution.py:53
  275.3 12.6 %collective-permute-done.66.got_ref = bf16[4,96,1536]{2,1,0:T(8,128)(2,1)S(1)} collective-permute-done((bf16[4,96,1536]{2,1,0:T(8,128)(2,1)S(1)}, bf16[4,96,1536]{2,1,0:T(8,128)(2,1)S(1)}, u32[]{:S(2)}, u32[]{:S(2)}) %collective-permute-start.66) | collective-permute-done | bytes 1179680 | tf_op jit(solution)/shard_map/ppermute | solution.py:49
  294.9 6.5 %collective-permute-done.56 = f32[36,384]{1,0:T(8,128)S(1)} collective-permute-done((f32[36,384]{1,0:T(8,128)S(1)}, f32[36,384]{1,0:T(8,128)S(1)}, u32[]{:S(2)}, u32[]{:S(2)}) %collective-permute-start.56) | collective-permute-done | bytes 55328 | tf_op jit(solution)/shard_map/ppermute | solution.py:796
  305.0 5.3 %collective-permute-done.57 = f32[36,384]{1,0:T(8,128)S(1)} collective-permute-done((f32[36,384]{1,0:T(8,128)S(1)}, f32[36,384]{1,0:T(8,128)S(1)}, u32[]{:S(2)}, u32[]{:S(2)}) %collective-permute-start.57) | collective-permute-done | bytes 55328 | tf_op jit(solution)/shard_map/ppermute | solution.py:796
  317.5 23.9 %collective-permute-done.58 = f32[36,384]{1,0:T(8,128)S(1)} collective-permute-done((f32[36,384]{1,0:T(8,128)S(1)}, f32[36,384]{1,0:T(8,128)S(1)}, u32[]{:S(2)}, u32[]{:S(2)}) %collective-permute-start.58) | collective-permute-done | bytes 55328 | tf_op jit(solution)/shard_map/ppermute | solution.py:796
  346.1 4.8 %collective-permute-done.68.refs_1_ = bf16[1,96,1536]{2,1,0:T(8,128)(2,1)S(1)} collective-permute-done((bf16[1,96,1536]{2,1,0:T(8,128)(2,1)S(1)}, bf16[1,96,1536]{2,1,0:T(8,128)(2,1)S(1)}, u32[]{:S(2)}, u32[]{:S(2)}) %collective-permute-start.68) | collective-permute-done | bytes 294944 | tf_op jit(solution)/shard_map/ppermute | solution.py:49
  (200 shorter events, 135.8 us)
Async XLA Ops:
  29.7 35.9 %collective-permute-start.6 = (bf16[4,192,384]{2,1,0:T(8,128)(2,1)S(1)}, bf16[4,192,384]{2,1,0:T(8,128)(2,1)S(1)}, u32[]{:S(2)}, u32[]{:S(2)}) collective-permute-start(bf16[4,192,384]{2,1,0:T(8,128)(2,1)S(1)} %join.15.refs_0_), channel_id=1, source_target_pairs={{0,2},{2,0},{4,6},{6,4},{8,10},{10,8},{12,14},{14,12},{16,18},{18,... | collective-permute-start | bytes 1769480 | tf_op jit(solution)/shard_map/ppermute | solution.py:49
  38.7 26.9 %collective-permute-start.7 = (bf16[4,192,384]{2,1,0:T(8,128)(2,1)S(1)}, bf16[4,192,384]{2,1,0:T(8,128)(2,1)S(1)}, u32[]{:S(2)}, u32[]{:S(2)}) collective-permute-start(bf16[4,192,384]{2,1,0:T(8,128)(2,1)S(1)} %collective-permute-done.5.refs_1_), channel_id=1, source_target_pairs={{0,2},{2,0},{4,6},{6,4},{8,10},{10,8},{12,14},{14,12},{16,18},{18,... | collective-permute-start | bytes 1769480 | tf_op jit(solution)/shard_map/ppermute | solution.py:49
  55.1 26.8 %collective-permute-start.15 = (bf16[4,48,1536]{2,1,0:T(8,128)(2,1)S(1)}, bf16[4,48,1536]{2,1,0:T(8,128)(2,1)S(1)}, u32[]{:S(2)}, u32[]{:S(2)}) collective-permute-start(bf16[4,48,1536]{2,1,0:T(8,128)(2,1)S(1)} %join.14.refs_0_), channel_id=1, source_target_pairs={{0,4},{2,6},{4,0},{6,2},{8,12},{10,14},{12,8},{14,10},{16,20},{18,... | collective-permute-start | bytes 1769480 | tf_op jit(solution)/shard_map/ppermute | solution.py:49
  60.7 21.2 %collective-permute-start.18 = (bf16[4,48,1536]{2,1,0:T(8,128)(2,1)S(1)}, bf16[4,48,1536]{2,1,0:T(8,128)(2,1)S(1)}, u32[]{:S(2)}, u32[]{:S(2)}) collective-permute-start(bf16[4,48,1536]{2,1,0:T(8,128)(2,1)S(1)} %join.17.refs_4_), channel_id=1, source_target_pairs={{0,4},{2,6},{4,0},{6,2},{8,12},{10,14},{12,8},{14,10},{16,20},{18,... | collective-permute-start | bytes 1769480 | tf_op jit(solution)/shard_map/ppermute | solution.py:49
  71.6 15.5 %collective-permute-start.16 = (bf16[4,48,1536]{2,1,0:T(8,128)(2,1)S(1)}, bf16[4,48,1536]{2,1,0:T(8,128)(2,1)S(1)}, u32[]{:S(2)}, u32[]{:S(2)}) collective-permute-start(bf16[4,48,1536]{2,1,0:T(8,128)(2,1)S(1)} %join.14.refs_0_), channel_id=1, source_target_pairs={{0,2},{2,0},{4,6},{6,4},{8,10},{10,8},{12,14},{14,12},{16,18},{18,... | collective-permute-start | bytes 1769480 | tf_op jit(solution)/shard_map/ppermute | solution.py:49
  79.8 14.6 %collective-permute-start.26 = (bf16[4,192,384]{2,1,0:T(8,128)(2,1)S(1)}, bf16[4,192,384]{2,1,0:T(8,128)(2,1)S(1)}, u32[]{:S(2)}, u32[]{:S(2)}) collective-permute-start(bf16[4,192,384]{2,1,0:T(8,128)(2,1)S(1)} %join.19.refs_0_), channel_id=1, source_target_pairs={{0,4},{2,6},{4,0},{6,2},{8,12},{10,14},{12,8},{14,10},{16,20},{18,... | collective-permute-start | bytes 1769480 | tf_op jit(solution)/shard_map/ppermute | solution.py:49
  81.9 15.0 %collective-permute-start.17 = (bf16[4,48,1536]{2,1,0:T(8,128)(2,1)S(1)}, bf16[4,48,1536]{2,1,0:T(8,128)(2,1)S(1)}, u32[]{:S(2)}, u32[]{:S(2)}) collective-permute-start(bf16[4,48,1536]{2,1,0:T(8,128)(2,1)S(1)} %collective-permute-done.15.refs_1_), channel_id=1, source_target_pairs={{0,2},{2,0},{4,6},{6,4},{8,10},{10,8},{12,14},{14,12},{16,18},{18,... | collective-permute-start | bytes 1769480 | tf_op jit(solution)/shard_map/ppermute | solution.py:49
  82.4 14.5 %collective-permute-start.20 = (bf16[4,48,1536]{2,1,0:T(8,128)(2,1)S(1)}, bf16[4,48,1536]{2,1,0:T(8,128)(2,1)S(1)}, u32[]{:S(2)}, u32[]{:S(2)}) collective-permute-start(bf16[4,48,1536]{2,1,0:T(8,128)(2,1)S(1)} %collective-permute-done.18.refs_5_), channel_id=1, source_target_pairs={{0,2},{2,0},{4,6},{6,4},{8,10},{10,8},{12,14},{14,12},{16,18},{18,... | collective-permute-start | bytes 1769480 | tf_op jit(solution)/shard_map/ppermute | solution.py:49
  94.4 26.0 %collective-permute-start.27 = (bf16[4,192,384]{2,1,0:T(8,128)(2,1)S(1)}, bf16[4,192,384]{2,1,0:T(8,128)(2,1)S(1)}, u32[]{:S(2)}, u32[]{:S(2)}) collective-permute-start(bf16[4,192,384]{2,1,0:T(8,128)(2,1)S(1)} %join.19.refs_0_), channel_id=1, source_target_pairs={{0,2},{2,0},{4,6},{6,4},{8,10},{10,8},{12,14},{14,12},{16,18},{18,... | collective-permute-start | bytes 1769480 | tf_op jit(solution)/shard_map/ppermute | solution.py:49
  94.4 26.0 %collective-permute-start.28 = (bf16[4,192,384]{2,1,0:T(8,128)(2,1)S(1)}, bf16[4,192,384]{2,1,0:T(8,128)(2,1)S(1)}, u32[]{:S(2)}, u32[]{:S(2)}) collective-permute-start(bf16[4,192,384]{2,1,0:T(8,128)(2,1)S(1)} %collective-permute-done.26.refs_1_), channel_id=1, source_target_pairs={{0,2},{2,0},{4,6},{6,4},{8,10},{10,8},{12,14},{14,12},{16,18},{18,... | collective-permute-start | bytes 1769480 | tf_op jit(solution)/shard_map/ppermute | solution.py:49
  105.4 14.9 %collective-permute-start.23 = (bf16[256,768]{1,0:T(8,128)(2,1)S(1)}, bf16[256,768]{1,0:T(8,128)(2,1)S(1)}, u32[]{:S(2)}, u32[]{:S(2)}) collective-permute-start(bf16[256,768]{1,0:T(8,128)(2,1)S(1)} %get-tuple-element.188.n_ref.n0_ref), channel_id=1, source_target_pairs={{0,1},{1,0},{2,3},{3,2},{4,5},{5,4},{6,7},{7,6},{8,9},{9,8},{10,11... | collective-permute-start | bytes 1179656 | tf_op jit(solution)/shard_map/ppermute | solution.py:53
  124.6 16.3 %collective-permute-start.34 = (bf16[4,48,1536]{2,1,0:T(8,128)(2,1)S(1)}, bf16[4,48,1536]{2,1,0:T(8,128)(2,1)S(1)}, u32[]{:S(2)}, u32[]{:S(2)}) collective-permute-start(bf16[4,48,1536]{2,1,0:T(8,128)(2,1)S(1)} %join.21.refs_0_), channel_id=1, source_target_pairs={{0,4},{2,6},{4,0},{6,2},{8,12},{10,14},{12,8},{14,10},{16,20},{18,... | collective-permute-start | bytes 1769480 | tf_op jit(solution)/shard_map/ppermute | solution.py:49
  126.1 23.7 %collective-permute-start.37 = (bf16[4,48,1536]{2,1,0:T(8,128)(2,1)S(1)}, bf16[4,48,1536]{2,1,0:T(8,128)(2,1)S(1)}, u32[]{:S(2)}, u32[]{:S(2)}) collective-permute-start(bf16[4,48,1536]{2,1,0:T(8,128)(2,1)S(1)} %join.23.refs_4_), channel_id=1, source_target_pairs={{0,4},{2,6},{4,0},{6,2},{8,12},{10,14},{12,8},{14,10},{16,20},{18,... | collective-permute-start | bytes 1769480 | tf_op jit(solution)/shard_map/ppermute | solution.py:49
  127.0 22.9 %collective-permute-start.12 = (bf16[256,768]{1,0:T(8,128)(2,1)S(1)}, bf16[256,768]{1,0:T(8,128)(2,1)S(1)}, u32[]{:S(2)}, u32[]{:S(2)}) collective-permute-start(bf16[256,768]{1,0:T(8,128)(2,1)S(1)} %get-tuple-element.192.n0_ref), channel_id=1, source_target_pairs={{0,1},{1,0},{2,3},{3,2},{4,5},{5,4},{6,7},{7,6},{8,9},{9,8},{10,11... | collective-permute-start | bytes 1179656 | tf_op jit(solution)/shard_map/ppermute | solution.py:53
  137.1 24.4 %collective-permute-start.35 = (bf16[4,48,1536]{2,1,0:T(8,128)(2,1)S(1)}, bf16[4,48,1536]{2,1,0:T(8,128)(2,1)S(1)}, u32[]{:S(2)}, u32[]{:S(2)}) collective-permute-start(bf16[4,48,1536]{2,1,0:T(8,128)(2,1)S(1)} %join.21.refs_0_), channel_id=1, source_target_pairs={{0,2},{2,0},{4,6},{6,4},{8,10},{10,8},{12,14},{14,12},{16,18},{18,... | collective-permute-start | bytes 1769480 | tf_op jit(solution)/shard_map/ppermute | solution.py:49
  140.8 20.7 %collective-permute-start.38 = (bf16[4,48,1536]{2,1,0:T(8,128)(2,1)S(1)}, bf16[4,48,1536]{2,1,0:T(8,128)(2,1)S(1)}, u32[]{:S(2)}, u32[]{:S(2)}) collective-permute-start(bf16[4,48,1536]{2,1,0:T(8,128)(2,1)S(1)} %join.23.refs_4_), channel_id=1, source_target_pairs={{0,2},{2,0},{4,6},{6,4},{8,10},{10,8},{12,14},{14,12},{16,18},{18,... | collective-permute-start | bytes 1769480 | tf_op jit(solution)/shard_map/ppermute | solution.py:49
  186.4 38.6 %collective-permute-start.47 = (bf16[4,96,1536]{2,1,0:T(8,128)(2,1)S(1)}, bf16[4,96,1536]{2,1,0:T(8,128)(2,1)S(1)}, u32[]{:S(2)}, u32[]{:S(2)}) collective-permute-start(bf16[4,96,1536]{2,1,0:T(8,128)(2,1)S(1)} %get-tuple-element.218), channel_id=1, source_target_pairs={{0,4},{2,6},{4,0},{6,2},{8,12},{10,14},{12,8},{14,10},{16,20},{18,... | collective-permute-start | bytes 3538952 | tf_op jit(solution)/shard_map/ppermute | solution.py:49
  210.6 17.3 %collective-permute-start.48 = (bf16[8,192,384]{2,1,0:T(8,128)(2,1)S(1)}, bf16[8,192,384]{2,1,0:T(8,128)(2,1)S(1)}, u32[]{:S(2)}, u32[]{:S(2)}) collective-permute-start(bf16[8,192,384]{2,1,0:T(8,128)(2,1)S(1)} %get-tuple-element.228), channel_id=1, source_target_pairs={{0,2},{2,0},{4,6},{6,4},{8,10},{10,8},{12,14},{14,12},{16,18},{18,... | collective-permute-start | bytes 3538952 | tf_op jit(solution)/shard_map/ppermute | solution.py:49
  232.0 16.3 %collective-permute-start.51 = (bf16[8,96,1536]{2,1,0:T(8,128)(2,1)S(1)}, bf16[8,96,1536]{2,1,0:T(8,128)(2,1)S(1)}, u32[]{:S(2)}, u32[]{:S(2)}) collective-permute-start(bf16[8,96,1536]{2,1,0:T(8,128)(2,1)S(1)} %get-tuple-element.246), channel_id=1, source_target_pairs={{0,2},{2,0},{4,6},{6,4},{8,10},{10,8},{12,14},{14,12},{16,18},{18,... | collective-permute-start | bytes 7077896 | tf_op jit(solution)/shard_map/ppermute | solution.py:49
  232.1 15.7 %collective-permute-start.52 = (bf16[2,96,1536]{2,1,0:T(8,128)(2,1)S(1)}, bf16[2,96,1536]{2,1,0:T(8,128)(2,1)S(1)}, u32[]{:S(2)}, u32[]{:S(2)}) collective-permute-start(bf16[2,96,1536]{2,1,0:T(8,128)(2,1)S(1)} %get-tuple-element.233), channel_id=1, source_target_pairs={{0,8},{2,10},{4,12},{6,14},{8,0},{10,2},{12,4},{14,6},{16,24},{18,... | collective-permute-start | bytes 1769480 | tf_op jit(solution)/shard_map/ppermute | solution.py:49
  232.5 15.7 %collective-permute-start.59 = (bf16[4,192,384]{2,1,0:T(8,128)(2,1)S(1)}, bf16[4,192,384]{2,1,0:T(8,128)(2,1)S(1)}, u32[]{:S(2)}, u32[]{:S(2)}) collective-permute-start(bf16[4,192,384]{2,1,0:T(8,128)(2,1)S(1)} %get-tuple-element.237), channel_id=1, source_target_pairs={{0,4},{2,6},{4,0},{6,2},{8,12},{10,14},{12,8},{14,10},{16,20},{18,... | collective-permute-start | bytes 1769480 | tf_op jit(solution)/shard_map/ppermute | solution.py:49
  259.0 28.8 %collective-permute-start.66 = (bf16[4,96,1536]{2,1,0:T(8,128)(2,1)S(1)}, bf16[4,96,1536]{2,1,0:T(8,128)(2,1)S(1)}, u32[]{:S(2)}, u32[]{:S(2)}) collective-permute-start(bf16[4,96,1536]{2,1,0:T(8,128)(2,1)S(1)} %get-tuple-element.248), channel_id=1, source_target_pairs={{0,4},{2,6},{4,0},{6,2},{8,12},{10,14},{12,8},{14,10},{16,20},{18,... | collective-permute-start | bytes 3538952 | tf_op jit(solution)/shard_map/ppermute | solution.py:49
  262.6 40.6 %collective-permute-start.61 = (bf16[4,192,384]{2,1,0:T(8,128)(2,1)S(1)}, bf16[4,192,384]{2,1,0:T(8,128)(2,1)S(1)}, u32[]{:S(2)}, u32[]{:S(2)}) collective-permute-start(bf16[4,192,384]{2,1,0:T(8,128)(2,1)S(1)} %get-tuple-element.282), channel_id=1, source_target_pairs={{0,4},{2,6},{4,0},{6,2},{8,12},{10,14},{12,8},{14,10},{16,20},{18,... | collective-permute-start | bytes 1769480 | tf_op jit(solution)/shard_map/ppermute | solution.py:49
  273.6 18.3 %collective-permute-start.54 = (f32[36,384]{1,0:T(8,128)S(1)}, f32[36,384]{1,0:T(8,128)S(1)}, u32[]{:S(2)}, u32[]{:S(2)}) collective-permute-start(f32[36,384]{1,0:T(8,128)S(1)} %get-tuple-element.267), channel_id=1, source_target_pairs={{0,1},{1,0},{2,3},{3,2},{4,5},{5,4},{6,7},{7,6},{8,9},{9,8},{10,11... | collective-permute-start | bytes 165896 | tf_op jit(solution)/shard_map/ppermute | solution.py:53
  288.2 23.9 %collective-permute-start.67 = (bf16[2,96,1536]{2,1,0:T(8,128)(2,1)S(1)}, bf16[2,96,1536]{2,1,0:T(8,128)(2,1)S(1)}, u32[]{:S(2)}, u32[]{:S(2)}) collective-permute-start(bf16[2,96,1536]{2,1,0:T(8,128)(2,1)S(1)} %get-tuple-element.293), channel_id=1, source_target_pairs={{0,8},{2,10},{4,12},{6,14},{8,0},{10,2},{12,4},{14,6},{16,24},{18,... | collective-permute-start | bytes 1769480 | tf_op jit(solution)/shard_map/ppermute | solution.py:49
  289.9 23.6 %collective-permute-start.32 = (bf16[256,768]{1,0:T(8,128)(2,1)S(1)}, bf16[256,768]{1,0:T(8,128)(2,1)S(1)}, u32[]{:S(2)}, u32[]{:S(2)}) collective-permute-start(bf16[256,768]{1,0:T(8,128)(2,1)S(1)} %get-tuple-element.196), channel_id=1, source_target_pairs={{0,1},{1,0},{2,3},{3,2},{4,5},{5,4},{6,7},{7,6},{8,9},{9,8},{10,11... | collective-permute-start | bytes 1179656 | tf_op jit(solution)/shard_map/ppermute | solution.py:53
  291.6 23.7 %collective-permute-start.64 = (bf16[2,192,384]{2,1,0:T(8,128)(2,1)S(1)}, bf16[2,192,384]{2,1,0:T(8,128)(2,1)S(1)}, u32[]{:S(2)}, u32[]{:S(2)}) collective-permute-start(bf16[2,192,384]{2,1,0:T(8,128)(2,1)S(1)} %get-tuple-element.272), channel_id=1, source_target_pairs={{0,8},{2,10},{4,12},{6,14},{8,0},{10,2},{12,4},{14,6},{16,24},{18,... | collective-permute-start | bytes 884744 | tf_op jit(solution)/shard_map/ppermute | solution.py:49
  303.2 41.3 %collective-permute-start.40 = (bf16[256,768]{1,0:T(8,128)(2,1)S(1)}, bf16[256,768]{1,0:T(8,128)(2,1)S(1)}, u32[]{:S(2)}, u32[]{:S(2)}) collective-permute-start(bf16[256,768]{1,0:T(8,128)(2,1)S(1)} %get-tuple-element.201), channel_id=1, source_target_pairs={{0,1},{1,0},{2,3},{3,2},{4,5},{5,4},{6,7},{7,6},{8,9},{9,8},{10,11... | collective-permute-start | bytes 1179656 | tf_op jit(solution)/shard_map/ppermute | solution.py:53
  310.3 31.1 %collective-permute-start.62 = (bf16[2,192,384]{2,1,0:T(8,128)(2,1)S(1)}, bf16[2,192,384]{2,1,0:T(8,128)(2,1)S(1)}, u32[]{:S(2)}, u32[]{:S(2)}) collective-permute-start(bf16[2,192,384]{2,1,0:T(8,128)(2,1)S(1)} %get-tuple-element.284), channel_id=1, source_target_pairs={{0,8},{2,10},{4,12},{6,14},{8,0},{10,2},{12,4},{14,6},{16,24},{18,... | collective-permute-start | bytes 884744 | tf_op jit(solution)/shard_map/ppermute | solution.py:49
  312.1 34.0 %collective-permute-start.69 = (bf16[1,96,1536]{2,1,0:T(8,128)(2,1)S(1)}, bf16[1,96,1536]{2,1,0:T(8,128)(2,1)S(1)}, u32[]{:S(2)}, u32[]{:S(2)}) collective-permute-start(bf16[1,96,1536]{2,1,0:T(8,128)(2,1)S(1)} %get-tuple-element.250), channel_id=1, source_target_pairs={{0,16},{2,18},{4,20},{6,22},{8,24},{10,26},{12,28},{14,30},{16,0},... | collective-permute-start | bytes 884744 | tf_op jit(solution)/shard_map/ppermute | solution.py:49
  313.6 27.8 %collective-permute-start.58 = (f32[36,384]{1,0:T(8,128)S(1)}, f32[36,384]{1,0:T(8,128)S(1)}, u32[]{:S(2)}, u32[]{:S(2)}) collective-permute-start(f32[36,384]{1,0:T(8,128)S(1)} %add.60), channel_id=1, source_target_pairs={{0,16},{2,18},{4,20},{6,22},{8,24},{10,26},{12,28},{14,30},{16,0},... | collective-permute-start | bytes 165896 | tf_op jit(solution)/shard_map/ppermute | solution.py:796
  315.3 35.6 %collective-permute-start.68 = (bf16[1,96,1536]{2,1,0:T(8,128)(2,1)S(1)}, bf16[1,96,1536]{2,1,0:T(8,128)(2,1)S(1)}, u32[]{:S(2)}, u32[]{:S(2)}) collective-permute-start(bf16[1,96,1536]{2,1,0:T(8,128)(2,1)S(1)} %get-tuple-element.295), channel_id=1, source_target_pairs={{0,16},{2,18},{4,20},{6,22},{8,24},{10,26},{12,28},{14,30},{16,0},... | collective-permute-start | bytes 884744 | tf_op jit(solution)/shard_map/ppermute | solution.py:49
  (54 other events, 468.2 us)
